TPU v7x, 512 devices: a whole 4x8x8 slice. The times are simulated.
512 devices in a mesh: frame: 16 (over x, y_lo, core), crop: 4 (over y_hi), dp: 8 (over z).
Axes of the slice: x: 4, y: 8 (y_hi: 4, y_lo: 2; y = y_hi * 2 + y_lo), z: 8, core: 2. Of those that a mesh axis runs over, the one named last changes fastest.
Arguments:
- global_clips: bfloat16 [8, 16, 256, 1408], P('dp', 'frame', 'crop'), may hold values from -6 to 6
- frame_map: int32 [8, 16, 8], P('dp', 'crop'), may hold values from 0 to 15
- teacher_qkv: bfloat16 [1408, 4224], P(None, 'frame'), may hold values from -0.15625 to 0.15625
- teacher_out: bfloat16 [1408, 1408], P('frame'), may hold values from -0.15625 to 0.15625
- teacher_bottle: bfloat16 [1408, 256], replicated, may hold values from -0.15625 to 0.15625
- student_qkv: bfloat16 [1408, 4224], P(None, 'frame'), may hold values from -0.15625 to 0.15625
- student_out: bfloat16 [1408, 1408], P('frame'), may hold values from -0.15625 to 0.15625
- student_bottle: bfloat16 [1408, 256], replicated, may hold values from -0.15625 to 0.15625
- prototypes: bfloat16 [256, 32768], P(None, 'frame'), may hold values from -1.796875 to 1.796875
- center: float32 [32768], P('frame'), may hold values from -8.6 to -3.9
Outputs:
- grad_qkv: float32 [1408, 4224], P(('crop', 'dp'), 'frame')
- grad_out: float32 [1408, 1408], P('frame', ('crop', 'dp'))
- grad_bottle: float32 [1408, 256], P(('crop', 'dp'))
All inputs are finite; a program needn't handle non-finite values.
Results may differ from a plain program's by a relative error of at most 0.00035.
Values may be sent and summed in bfloat16 or wider, within the bound.
No kernel may reach another device: no remote copies, remote signals or barrier semaphores. Data moves between devices by JAX's collectives and lax.ppermute only.
A program may use at most 64 MiB of HBM per device.

v0:
```python
import functools
import math

import jax
import jax.numpy as jnp
from jax import lax
from jax.experimental import pallas as pl
from jax.experimental.pallas import tpu as pltpu
from jax.sharding import PartitionSpec as P


D = 1408
HS = 88
FRAMES = 16
BOTTLE = 256
GP = 8
ROWS = FRAMES * GP
TILES = 4
LFRAMES = 8
CLIPS = 4
NTOK = 512
NTEACH = 4096
TAU_TEACH = 0.04
TAU_STUD = 0.1
ALL_CLIPS = 16
HIGH = lax.Precision.HIGHEST
F32 = jnp.float32
BF16 = jnp.bfloat16
NEG = -1e30
SCALE = 1.0 / math.sqrt(HS)
MSG = 24
QROWS = 56
STEP = 64.0
INTERPRET = False

NN = (((1,), (0,)), ((), ()))
NT = (((1,), (1,)), ((), ()))
TN = (((0,), (0,)), ((), ()))


def call(kernel, outs, *args, scratch=(), smem=0, hbm_in=(), hbm_out=(), limit=16):
    def space(index, in_hbm):
        return pl.BlockSpec(memory_space=pltpu.HBM if index in in_hbm else pltpu.VMEM)

    spec = [pl.BlockSpec(memory_space=pltpu.SMEM)] * smem
    spec += [space(index, hbm_in) for index in range(smem, len(args))]
    args = [pltpu.with_memory_space_constraint(arg, pltpu.HBM) if index in hbm_in else arg for index, arg in enumerate(args)]
    return pl.pallas_call(
        kernel,
        out_shape=tuple(
            pltpu.HBM(shape, dtype) if index in hbm_out else jax.ShapeDtypeStruct(shape, dtype)
            for index, (shape, dtype) in enumerate(outs)
        ),
        in_specs=spec,
        out_specs=tuple(space(index, hbm_out) for index in range(len(outs))),
        scratch_shapes=list(scratch),
        compiler_params=pltpu.CompilerParams(vmem_limit_bytes=limit * 2**20),
        interpret=INTERPRET,
    )(*args)


def room(*arrays):
    held = [pltpu.VMEM(tuple(array.shape), array.dtype) for array in arrays]
    return held + [pltpu.SemaphoreType.DMA((len(held),))]


def begin(sources, targets, sems):
    copies = [pltpu.make_async_copy(source, target, sems.at[i]) for i, (source, target) in enumerate(zip(sources, targets))]
    for copy in copies:
        copy.start()
    return copies


def mm(a, b, dims=NN):
    return lax.dot_general(a, b, dims, preferred_element_type=F32)


def mmh(a, b, dims=NN):
    return lax.dot_general(a, b, dims, precision=HIGH, preferred_element_type=F32)


def pieces(x):
    top = x.astype(BF16)
    rest = x - top.astype(F32)
    mid = rest.astype(BF16)
    return top, mid, (rest - mid.astype(F32)).astype(BF16)


def mm3(x, y, dims=NN):
    top, mid, low = pieces(x)
    return mm(top, y, dims) + (mm(mid, y, dims) + mm(low, y, dims))


def rsqrt(x):
    guess = lax.rsqrt(x)
    return guess * (1.5 - 0.5 * x * guess * guess)


def same_patch():
    row = lax.broadcasted_iota(jnp.int32, (ROWS, ROWS), 0)
    col = lax.broadcasted_iota(jnp.int32, (ROWS, ROWS), 1)
    return jnp.where((row % GP) == (col % GP), 0.0, NEG).astype(F32)


def split_qkv(flat):
    rounded = flat.astype(BF16)
    return rounded[:, :HS], rounded[:, HS : 2 * HS], rounded[:, 2 * HS :]


def spread_kernel(tok, out):
    half = out.shape[1]
    for peer in range(FRAMES):
        out[peer] = tok[(peer % 2) * half : (peer % 2 + 1) * half, :]


def prep_kernel(
    maps, frame, tok, t_out, t_oth, s_out, s_oth, t_bot, s_bot, mt, ms, otz, zlocal, plocal, ccol, crow
):
    total = jnp.sum(tok[...].astype(F32), axis=0, keepdims=True)
    otz[...] = mm3(total, t_bot[...])
    osz = mm3(total, s_bot[...])
    mt[0] = mm(t_out[...], t_bot[...])
    mt[1] = mm(t_oth[...], t_bot[...])
    ms[0] = mm(s_out[...], s_bot[...])
    ms[1] = mm(s_oth[...], s_bot[...])
    lane = lax.broadcasted_iota(jnp.int32, (1, ROWS), 1)
    row = lax.broadcasted_iota(jnp.int32, (ROWS, ROWS), 0) // GP
    down = jnp.zeros((ROWS, ROWS), F32)
    across = [jnp.zeros((1, ROWS), F32) for _ in range(CLIPS)]
    mine = [jnp.zeros((1, ROWS), F32) for _ in range(CLIPS)]
    for step in range(LFRAMES):
        shown = jnp.full((1, ROWS), -1, jnp.int32)
        for clip in range(CLIPS):
            index = maps[clip, step]
            shown = jnp.where(lane == clip, index, shown)
            across[clip] = across[clip] + jnp.where(lane // GP == index, 1.0, 0.0)
            mine[clip] = mine[clip] + jnp.where(index == frame[0], 1.0, 0.0)
        down = down + jnp.where(row == shown, 1.0, 0.0)
    crow[...] = down
    for clip in range(CLIPS):
        ccol[clip : clip + 1, :] = across[clip]
        frac = mine[clip][:, 0:1] / NTOK
        zlocal[clip : clip + 1, :] = frac * osz
        plocal[clip : clip + 1, :] = frac * total


def teacher_kernel(x, w_own_far, w_oth_far, mt_far, otz, normed, zt, w_own, w_oth, mt, sems):
    copies = begin((w_own_far, w_oth_far, mt_far), (w_own, w_oth, mt), sems)
    for group in range(2):
        values = x[:, group * 2 * GP : (group + 1) * 2 * GP, :].astype(F32)
        middle = jnp.mean(values, axis=-1, keepdims=True)
        moved = values - middle
        spread = jnp.mean(moved * moved, axis=-1, keepdims=True)
        token = moved * rsqrt(spread + 1e-06)
        normed[2 * group] = token[:, :GP].reshape(ROWS, D).astype(BF16)
        normed[2 * group + 1] = token[:, GP:].reshape(ROWS, D).astype(BF16)
    mask = same_patch()
    tokens = normed[...].reshape(TILES * ROWS, D)
    total = otz[...]
    copies[2].wait()
    for head, weight in enumerate((w_own, w_oth)):
        copies[head].wait()
        flat = mm(tokens, weight[...], NT)
        summed = jnp.zeros((1, HS), F32)
        for tile in range(TILES):
            query, key, value = split_qkv(flat[tile * ROWS : (tile + 1) * ROWS])
            scores = mm(query, key, NT) * SCALE + mask
            scores = jnp.exp(scores - jnp.max(scores, axis=-1, keepdims=True))
            share = scores / jnp.sum(scores, axis=-1, keepdims=True)
            att = mm(share.astype(BF16), value)
            summed = summed + jnp.sum(att, axis=0, keepdims=True)
        total = total + mmh(summed, mt[head])
    for crop in range(zt.shape[0]):
        zt[crop] = total / NTEACH


def clip_shares(scores, count):
    here = jnp.where(count > 0.0, scores, NEG)
    here = jnp.exp(here - jnp.max(here, axis=-1, keepdims=True))
    return here / jnp.sum(here * count, axis=-1, keepdims=True)


def student_kernel(
    normed, w_own_far, w_oth_far, ms_far, s_out_far, s_oth_far, zlocal, plocal, ccol, crow,
    own_far, oth_far, shares_own_far, shares_oth_far, zs, pooled, heads,
    w_own, w_oth, ms, s_out, s_oth, sems, own, oth, shares_own, shares_oth, out_sems,
):
    copies = begin((w_own_far, w_oth_far, ms_far, s_out_far, s_oth_far), (w_own, w_oth, ms, s_out, s_oth), sems)
    mask = same_patch()
    tokens = normed[...].reshape(TILES * ROWS, D)
    leaving = []
    sides = ((w_own, own, shares_own, own_far, shares_own_far), (w_oth, oth, shares_oth, oth_far, shares_oth_far))
    for head, (weight, keep, shares, keep_far, shares_far) in enumerate(sides):
        copies[head].wait()
        flat = mm(tokens, weight[...], NT)
        summed = jnp.zeros((CLIPS, HS), F32)
        for tile in range(TILES):
            query, key, value = split_qkv(flat[tile * ROWS : (tile + 1) * ROWS])
            keep[0, tile] = query
            keep[1, tile] = key
            keep[2, tile] = value
            scores = mm(query, key, NT) * SCALE + mask
            totals = []
            for clip in range(CLIPS):
                count = ccol[clip : clip + 1, :]
                share = clip_shares(scores, count)
                shares[tile, clip] = share
                share = share.astype(BF16).astype(F32) * crow[:, clip : clip + 1]
                totals.append(jnp.sum(share, axis=0, keepdims=True) * count)
            summed = summed + mm3(jnp.concatenate(totals, axis=0), value)
        leaving += begin((keep, shares), (keep_far, shares_far), out_sems.at[pl.ds(2 * head, 2)])
        heads[head] = summed / NTOK
    for copy in copies[2:]:
        copy.wait()
    zs[...] = mmh(heads[0], ms[0]) + mmh(heads[1], ms[1]) + zlocal[...]
    pooled[...] = mm3(heads[0], s_out[...]) + mm3(heads[1], s_oth[...]) + plocal[...]
    for copy in leaving:
        copy.wait()


def flip_kernel(normed_far, normed_oth_far, out_own_far, out_oth_far, half, half_oth, sems, out_own, out_oth, out_sems):
    copies = begin((normed_far, normed_oth_far), (half, half_oth), sems)
    leaving = []
    for index, (held, out, far) in enumerate(((half, out_own, out_own_far), (half_oth, out_oth, out_oth_far))):
        copies[index].wait()
        out[...] = jnp.transpose(held[...].reshape(TILES * ROWS, D))
        leaving += begin((out,), (far,), out_sems.at[pl.ds(index, 1)])
    for copy in leaving:
        copy.wait()


def message_kernel(frame, zs, ztc, pooled, heads, out):
    me = frame[0]
    zt = jnp.sum(ztc[...], axis=0)
    for peer in range(FRAMES):
        out[peer, 0:4, :] = zs[:, 0:128]
        out[peer, 4:8, :] = zs[:, 128:256]
        out[peer, 8:9, :] = zt[:, 0:128]
        out[peer, 9:10, :] = zt[:, 128:256]
        out[peer, 10:MSG, :] = jnp.zeros((MSG - 10, 128), F32)
        out[peer, 10:14, 0:HS] = pooled[:, peer * HS : (peer + 1) * HS]
        mine = (me == peer).astype(F32)
        partner = (jnp.bitwise_xor(me, 1) == peer).astype(F32)
        out[peer, 14:18, 0:HS] = heads[0] * mine + heads[1] * partner


def logits_kernel(got, protos, center, out, zs, heads):
    total = got[0]
    for source in range(1, FRAMES):
        total = total + got[source]
    z_s = jnp.concatenate([total[0:4], total[4:8]], axis=1)
    z_t = jnp.concatenate([total[8:9], total[9:10]], axis=1)
    zs[...] = z_s
    heads[...] = total[14:18, 0:HS]
    z_all = jnp.concatenate([z_s, z_t], axis=0)
    unit = z_all * rsqrt(jnp.sum(z_all * z_all, axis=-1, keepdims=True) + 1e-06)
    wide = mm3(unit, protos[...])
    logits = jnp.concatenate([wide[0:4] / TAU_STUD, (wide[4:5] - center[...]) / TAU_TEACH], axis=0)
    top = jnp.max(logits, axis=-1, keepdims=True)
    grown = jnp.exp(logits - top)
    size = jnp.sum(grown, axis=-1, keepdims=True)
    vec = mm3(grown, protos[...], NT)
    lane = lax.broadcasted_iota(jnp.int32, (5, 128), 1)
    tops = jnp.where(lane == 0, top, jnp.where(lane == 1, size, 0.0))
    for peer in range(FRAMES):
        out[peer, 0:5, :] = vec[:, 0:128]
        out[peer, 5:10, :] = vec[:, 128:256]
        out[peer, 10:15, :] = tops
        out[peer, 15:19, :] = total[10:14]
        out[peer, 19:MSG, :] = jnp.zeros((MSG - 19, 128), F32)


def code_of(peak):
    return jnp.ceil(jnp.log(jnp.maximum(peak, 1e-30)) * (STEP / math.log(2.0))) + 1.0


def scale_of(code):
    return jnp.exp(code * (math.log(2.0) / STEP))


def whole_max(x):
    return jnp.max(jnp.max(x, axis=-1, keepdims=True), axis=0, keepdims=True)


def stack3(parts):
    return jnp.concatenate([piece for part in parts for piece in pieces(part)], axis=0)


def back_kernel(
    peers, got, zs, heads, ms, own_far, oth_far, shares_own_far, shares_oth_far,
    ccol, crow, flip_own_far, flip_oth_far, out_far,
    keep_own, shares_own, keep_oth, shares_oth, flip, sems, out, out_sems, grad, rhs, last, line,
):
    count = TILES * ROWS
    copies = begin(
        (own_far, shares_own_far, oth_far, shares_oth_far, flip_own_far, flip_oth_far),
        (keep_own, shares_own, keep_oth, shares_oth, flip.at[:, pl.ds(0, count)], flip.at[:, pl.ds(count, count)]),
        sems,
    )
    tops = [got[source, 10:15, 0:1] for source in range(FRAMES)]
    top = functools.reduce(jnp.maximum, tops)
    size = jnp.zeros((5, 1), F32)
    low = jnp.zeros((5, 128), F32)
    high = jnp.zeros((5, 128), F32)
    for source in range(FRAMES):
        factor = jnp.exp(tops[source] - top)
        size = size + got[source, 10:15, 1:2] * factor
        low = low + got[source, 0:5, :] * factor
        high = high + got[source, 5:10, :] * factor
    expect = jnp.concatenate([low, high], axis=1) / size
    d_unit = (expect[0:4] - expect[4:5]) / (ALL_CLIPS * TAU_STUD)
    z_s = zs[...]
    inverse = rsqrt(jnp.sum(z_s * z_s, axis=-1, keepdims=True) + 1e-06)
    unit = z_s * inverse
    d_z = (d_unit - unit * jnp.sum(unit * d_unit, axis=-1, keepdims=True)) * inverse
    d_heads = mmh(d_z, ms[0], NT) / NTOK
    lane = lax.broadcasted_iota(jnp.int32, (ROWS, ROWS), 1)
    for half, (keep, shares) in enumerate(((keep_own, shares_own), (keep_oth, shares_oth))):
        copies[2 * half].wait()
        copies[2 * half + 1].wait()
        for tile in range(TILES):
            d_weights = mm3(d_heads, keep[2, tile], NT).astype(BF16).astype(F32)
            taken = [
                jnp.sum(shares[tile, clip].astype(BF16).astype(F32) * crow[:, clip : clip + 1], axis=0, keepdims=True)
                for clip in range(CLIPS)
            ]
            d_down = jnp.transpose(jnp.concatenate([d_weights] + taken, axis=0))
            inner = jnp.zeros((ROWS, ROWS), F32)
            grow_q = []
            for clip in range(CLIPS):
                share = shares[tile, clip] * ccol[clip : clip + 1, :]
                d_w = d_weights[clip : clip + 1, :]
                mean = jnp.sum(share * d_w, axis=-1, keepdims=True)
                inner = jnp.where(lane == clip, mean, inner)
                grow_q.append(share * (d_w - mean) * SCALE)
            inner = jnp.transpose(inner)
            grow_k = [
                jnp.transpose(shares[tile, clip])
                * ccol[clip : clip + 1, :]
                * (d_down[:, clip : clip + 1] - inner[clip : clip + 1, :])
                * SCALE
                for clip in range(CLIPS)
            ]
            wide_q = mm(stack3(grow_q), keep[1, tile])
            wide_k = mm(stack3(grow_k), keep[0, tile])
            totals = [jnp.zeros((ROWS, HS), F32) for _ in range(3)]
            for clip in range(CLIPS):
                many = crow[:, clip : clip + 1]
                first = 3 * clip * ROWS
                parts = [
                    wide[first : first + ROWS] + (wide[first + ROWS : first + 2 * ROWS] + wide[first + 2 * ROWS : first + 3 * ROWS])
                    for wide in (wide_q, wide_k)
                ]
                parts.append(d_down[:, CLIPS + clip : CLIPS + clip + 1] * d_heads[clip : clip + 1, :])
                totals = [total + many * part.astype(BF16).astype(F32) for total, part in zip(totals, parts)]
            packed = jnp.concatenate(totals, axis=1)
            first = packed.astype(BF16)
            second = (packed - first.astype(F32)).astype(BF16)
            rows = pl.ds((half * TILES + tile) * ROWS, ROWS)
            rhs[rows, 0:256] = first[:, 0:256]
            rhs[rows, 256:512] = second[:, 0:256]
            rhs[rows, 512:528] = jnp.concatenate([first[:, 256:264], second[:, 256:264]], axis=1)
    copies[4].wait()
    copies[5].wait()
    wide = mm(flip[...], rhs[...])
    main = wide[:, 0:256] + wide[:, 256:512]
    thin = jnp.transpose(wide[:, 512:520] + wide[:, 520:528])
    code = code_of(jnp.max(jnp.abs(main), axis=0, keepdims=True))
    grad[...] = jnp.round(main * (32000.0 / scale_of(code)))
    code_thin = code_of(jnp.max(jnp.abs(thin), axis=-1, keepdims=True))
    last[...] = jnp.round(thin * (32000.0 / scale_of(code_thin)))
    code_z = code_of(whole_max(jnp.abs(d_z)))
    sent_z = jnp.round(d_z * (32000.0 / scale_of(code_z)))
    mine = heads[...]
    code_h = code_of(whole_max(jnp.abs(mine)))
    sent_h = jnp.round(mine * (32000.0 / scale_of(code_h)))
    pooled = jnp.concatenate([got[source, 15:19, 0:HS] for source in range(FRAMES)], axis=1)
    code_p = code_of(whole_max(jnp.abs(pooled)))
    sent_p = jnp.round(pooled * (32000.0 / scale_of(code_p)))
    lane = lax.broadcasted_iota(jnp.int32, (1, 128), 1)
    codes = jnp.where(lane == 64, code_z, jnp.where(lane == 65, code_h, jnp.where(lane == 66, code_p, 0.0)))
    block = D // peers
    line[...] = jnp.zeros((QROWS, 256), F32)
    line[44:48, :] = sent_z
    line[48:49, 0:HS] = sent_h[0:1]
    line[48:49, 128 : 128 + HS] = sent_h[1:2]
    line[49:50, 0:HS] = sent_h[2:3]
    line[49:50, 128 : 128 + HS] = sent_h[3:4]
    line[55:56, :] = code
    leaving = []
    for peer in range(peers):
        line[0:block, :] = grad[peer * block : (peer + 1) * block, :]
        part = sent_p[:, peer * block : (peer + 1) * block]
        line[50:54, 0:block] = part
        thin_part = last[:, peer * block : (peer + 1) * block]
        line[50:54, 64 : 64 + block] = thin_part[0:4]
        line[50:54, 128 : 128 + block] = thin_part[4:8]
        line[50:54, 192:193] = code_thin[0:4]
        line[50:54, 193:194] = code_thin[4:8]
        line[54:55, 0:128] = codes
        out[peer] = line[...].astype(jnp.int32).astype(jnp.int16)
        leaving += begin((out.at[peer],), (out_far.at[peer],), out_sems.at[pl.ds(peer, 1)])
    for copy in leaving:
        copy.wait()


def final_kernel(peers, got, bottle, g_qkv, g_out, g_bottle, z_all, h_all, p_all):
    block = D // peers
    main = jnp.zeros((block, 256), F32)
    thin_a = jnp.zeros((4, block), F32)
    thin_b = jnp.zeros((4, block), F32)
    for source in range(peers):
        line = got[source].astype(jnp.int32).astype(F32)
        main = main + line[0:block] * (scale_of(line[55:56]) / 32000.0)
        thin_a = thin_a + line[50:54, 64 : 64 + block] * (scale_of(line[50:54, 192:193]) / 32000.0)
        thin_b = thin_b + line[50:54, 128 : 128 + block] * (scale_of(line[50:54, 193:194]) / 32000.0)
        scales = scale_of(line[54:55, 0:128]) / 32000.0
        first = source * CLIPS
        z_all[first : first + 4, :] = line[44:48] * scales[:, 64:65]
        scale_h = scales[:, 65:66]
        h_all[first : first + 1, :] = line[48:49, 0:HS] * scale_h
        h_all[first + 1 : first + 2, :] = line[48:49, 128 : 128 + HS] * scale_h
        h_all[first + 2 : first + 3, :] = line[49:50, 0:HS] * scale_h
        h_all[first + 3 : first + 4, :] = line[49:50, 128 : 128 + HS] * scale_h
        p_all[first : first + 4, :] = line[50:54, 0:block] * scales[:, 66:67]
    g_qkv[:, 0:256] = main
    g_qkv[:, 256:264] = jnp.transpose(jnp.concatenate([thin_a, thin_b], axis=0))
    d_z = z_all[...]
    g_bottle[...] = mmh(p_all[...], d_z, TN)
    g_out[...] = mmh(bottle[...].astype(F32), mmh(h_all[...], d_z, TN), NT)


def local(
    global_clips,
    frame_map,
    teacher_qkv,
    teacher_out,
    teacher_bottle,
    student_qkv,
    student_out,
    student_bottle,
    prototypes,
    center,
):
    frame = lax.axis_index("frame")
    peers = lax.axis_size("crop") * lax.axis_size("dp")
    crops = lax.axis_size("crop")
    swap = [(index, index ^ 1) for index in range(FRAMES)]
    tokens = global_clips[0, 0]
    (spread,) = call(
        spread_kernel,
        [((FRAMES, tokens.shape[0] // 2, D), BF16)],
        tokens,
    )
    mixed = lax.all_to_all(spread, "frame", 0, 0, tiled=True)
    t_own = teacher_qkv.T
    s_own = student_qkv.T
    t_oth = lax.ppermute(t_own, "frame", swap)
    s_oth = lax.ppermute(s_own, "frame", swap)
    t_out_oth = lax.ppermute(teacher_out, "frame", swap)
    s_out_oth = lax.ppermute(student_out, "frame", swap)
    mt, ms, otz, zlocal, plocal, ccol, crow = call(
        prep_kernel,
        [
            ((2, HS, BOTTLE), F32),
            ((2, HS, BOTTLE), F32),
            ((1, BOTTLE), F32),
            ((CLIPS, BOTTLE), F32),
            ((CLIPS, D), F32),
            ((CLIPS, ROWS), F32),
            ((ROWS, ROWS), F32),
        ],
        frame_map[0], frame.astype(jnp.int32).reshape(1),
        tokens, teacher_out, t_out_oth, student_out, s_out_oth, teacher_bottle, student_bottle,
        smem=2,
    )
    normed, zt = call(
        teacher_kernel,
        [((TILES, ROWS, D), BF16), ((crops, 1, BOTTLE), F32)],
        mixed, t_own, t_oth, mt, otz,
        hbm_in=(1, 2, 3), scratch=room(t_own, t_oth, mt),
    )
    ztc = lax.all_to_all(zt, "crop", 0, 0, tiled=True)
    keep = jax.ShapeDtypeStruct((3, TILES, ROWS, HS), BF16)
    table = jax.ShapeDtypeStruct((TILES, CLIPS, ROWS, ROWS), F32)
    own, oth, shares_own, shares_oth, zs, pooled, heads = call(
        student_kernel,
        [
            (keep.shape, BF16),
            (keep.shape, BF16),
            (table.shape, F32),
            (table.shape, F32),
            ((CLIPS, BOTTLE), F32),
            ((CLIPS, D), F32),
            ((2, CLIPS, HS), F32),
        ],
        normed, s_own, s_oth, ms, student_out, s_out_oth, zlocal, plocal, ccol, crow,
        hbm_in=(1, 2, 3, 4, 5), hbm_out=(0, 1, 2, 3), limit=20,
        scratch=room(s_own, s_oth, ms, student_out, s_out_oth) + room(keep, keep, table, table),
    )
    (sent,) = call(
        message_kernel,
        [((FRAMES, MSG, 128), F32)],
        frame.astype(jnp.int32).reshape(1), zs, ztc, pooled, heads, smem=1,
    )
    sent, leaving = lax.optimization_barrier((sent, (normed, oth, shares_oth)))
    got = lax.all_to_all(sent, "frame", 0, 0, tiled=True)
    normed_oth = lax.ppermute(leaving[0], "frame", swap)
    shares_got = lax.ppermute(leaving[2], "frame", swap)
    kept_oth = lax.ppermute(leaving[1], "frame", swap)
    flat = jax.ShapeDtypeStruct((D, TILES * ROWS), BF16)
    flips = call(
        flip_kernel,
        [(flat.shape, BF16), (flat.shape, BF16)],
        normed, normed_oth,
        hbm_in=(0, 1), hbm_out=(0, 1), scratch=room(normed, normed_oth) + room(flat, flat),
    )
    sent, z_s, my_heads = call(
        logits_kernel,
        [((FRAMES, MSG, 128), F32), ((CLIPS, BOTTLE), F32), ((CLIPS, HS), F32)],
        got, prototypes, center.reshape(1, -1),
    )
    got = lax.all_to_all(sent, "frame", 0, 0, tiled=True)
    (sent,) = call(
        functools.partial(back_kernel, peers),
        [((peers, QROWS, 256), jnp.int16)],
        got, z_s, my_heads, ms, own, kept_oth, shares_own, shares_got, ccol, crow, flips[0], flips[1],
        hbm_in=(4, 5, 6, 7, 10, 11), hbm_out=(0,), limit=30,
        scratch=room(own, shares_own, kept_oth, shares_got)[:-1]
        + [
            pltpu.VMEM((D, 2 * TILES * ROWS), BF16),
            pltpu.SemaphoreType.DMA((6,)),
            pltpu.VMEM((peers, QROWS, 256), jnp.int16),
            pltpu.SemaphoreType.DMA((peers,)),
            pltpu.VMEM((D, 256), F32),
            pltpu.VMEM((2 * TILES * ROWS, 528), BF16),
            pltpu.VMEM((8, D), F32),
            pltpu.VMEM((QROWS, 256), F32),
        ],
    )
    got = lax.all_to_all(sent, ("crop", "dp"), 0, 0, tiled=True)
    block = D // peers
    place = lax.axis_index("crop") * lax.axis_size("dp") + lax.axis_index("dp")
    bottle = lax.dynamic_slice_in_dim(student_bottle, place * block, block, axis=0)
    g_qkv, g_out, g_bottle = call(
        functools.partial(final_kernel, peers),
        [((block, 3 * HS), F32), ((block, HS), F32), ((block, BOTTLE), F32)],
        got, bottle,
        scratch=[
            pltpu.VMEM((peers * CLIPS, BOTTLE), F32),
            pltpu.VMEM((peers * CLIPS, HS), F32),
            pltpu.VMEM((peers * CLIPS, block), F32),
        ],
    )
    return g_qkv, g_out.T, g_bottle


def solution(mesh):
    return program(mesh)


def program(mesh):
    return jax.shard_map(
        local,
        mesh=mesh,
        in_specs=(
            P("dp", "frame", "crop", None),
            P("dp", "crop", None),
            P(None, "frame"),
            P("frame", None),
            P(),
            P(None, "frame"),
            P("frame", None),
            P(),
            P(None, "frame"),
            P("frame"),
        ),
        out_specs=(P(("crop", "dp"), "frame"), P("frame", ("crop", "dp")), P(("crop", "dp"), None)),
        check_vma=False,
    )
```

profile of v0, /device:TPU:78, one launch (start us, length us, event | category | flops | bytes accessed | tf_op | source)
XLA Modules:
  0.0 136.6 jit_solution(8145727344067581021)
XLA Ops:
  1.6 1.2 shard_map.121
  2.8 5.8 %all-to-all-start = ((bf16[16,32,1408]{2,1,0:T(8,128)(2,1)}), bf16[16,32,1408]{2,1,0:T(8,128)(2,1)S(1)}, u32[]{:S(2)}, u32[]{:S(2)}) async-start(bf16[16,32,1408]{2,1,0:T(8,128)(2,1)} %shard_map.121), calls=%async_computation | async-start | bytes 2883584 | tf_op jit(solution)/shard_map/all_to_all | solution.py:455
  8.7 2.0 %collective-permute-start = (bf16[264,1408]{1,0:T(8,128)(2,1)}, bf16[264,1408]{1,0:T(8,128)(2,1)}, u32[]{:S(2)}, u32[]{:S(2)}) collective-permute-start(bf16[264,1408]{1,0:T(8,128)(2,1)} %bitcast.11), channel_id=1, source_target_pairs={{0,32},{32,0},{64,96},{96,64},{128,160},{160,128},{192,224},{224,1... | collective-permute-start | bytes 2230280 | tf_op jit(solution)/shard_map/ppermute | solution.py:458
  10.7 2.3 %collective-permute-start.3 = (bf16[264,1408]{1,0:T(8,128)(2,1)}, bf16[264,1408]{1,0:T(8,128)(2,1)}, u32[]{:S(2)}, u32[]{:S(2)}) collective-permute-start(bf16[264,1408]{1,0:T(8,128)(2,1)} %bitcast.13), channel_id=1, source_target_pairs={{0,32},{32,0},{64,96},{96,64},{128,160},{160,128},{192,224},{224,1... | collective-permute-start | bytes 2230280 | tf_op jit(solution)/shard_map/ppermute | solution.py:459
  13.0 2.0 %collective-permute-start.2 = (bf16[88,1408]{1,0:T(8,128)(2,1)S(1)}, bf16[88,1408]{1,0:T(8,128)(2,1)S(1)}, u32[]{:S(2)}, u32[]{:S(2)}) collective-permute-start(bf16[88,1408]{1,0:T(8,128)(2,1)S(1)} %copy-done.2), channel_id=1, source_target_pairs={{0,32},{32,0},{64,96},{96,64},{128,160},{160,128},{192,224},{224,1... | collective-permute-start | bytes 743432 | tf_op jit(solution)/shard_map/ppermute | solution.py:461
  15.0 2.3 %collective-permute-start.1 = (bf16[88,1408]{1,0:T(8,128)(2,1)S(1)}, bf16[88,1408]{1,0:T(8,128)(2,1)S(1)}, u32[]{:S(2)}, u32[]{:S(2)}) collective-permute-start(bf16[88,1408]{1,0:T(8,128)(2,1)S(1)} %copy-done.10), channel_id=1, source_target_pairs={{0,32},{32,0},{64,96},{96,64},{128,160},{160,128},{192,224},{224,1... | collective-permute-start | bytes 743432 | tf_op jit(solution)/shard_map/ppermute | solution.py:460
  17.4 1.1 collective-permute-done.1.t_oth
  18.5 1.1 copy-done.9
  19.6 1.8 %shard_map.122 = (f32[2,88,256]{2,1,0:T(8,128)S(1)}, f32[2,88,256]{2,1,0:T(8,128)S(1)}, f32[1,256]{1,0:T(1,128)S(1)}, f32[4,256]{1,0:T(4,128)S(1)}, f32[4,1408]{...) custom-call(s32[4,8]{1,0:T(4,128)S(1)} %bitcast.10, s32[1]{0:T(128)} %bitcast.frame, ...), custom_call_target="tpu_custom_call" | custom-call | tf_op jit(solution)/shard_map/pallas_call | solution.py:48
  22.7 3.2 %all-to-all-done.x = bf16[16,32,1408]{2,1,0:T(8,128)(2,1)S(1)} async-done(((bf16[16,32,1408]{2,1,0:T(8,128)(2,1)}), bf16[16,32,1408]{2,1,0:T(8,128)(2,1)S(1)}, u32[]{:S(2)}, u32[]{:S(2)}) %all-to-all-start) | async-done | bytes 1441824 | tf_op jit(solution)/shard_map/all_to_all | solution.py:455
  26.0 6.7 %shard_map.123 = (bf16[4,128,1408]{2,1,0:T(8,128)(2,1)S(1)}, f32[4,1,256]{2,1,0:T(1,128)}) custom-call(bf16[16,32,1408]{2,1,0:T(8,128)(2,1)S(1)} %all-to-all-done.x, bf16[264,1408]{1,0:T(8,128)(2,1)} %bitcast.12, bf16[264,1408]{1,0:T(8,128)(2,1)} %collective-permute-done.w_oth_far, f32[2,88,256]{2,1,0:T(8,128)} %copy-done.11, f32[1,256]{1,0:T(1,128)S(1)} %get-tuple-element.32.otz), custom_call_target="tpu_custom_call" | custom-call | tf_op jit(solution)/shard_map/pallas_call | solution.py:48
  32.7 6.2 %all-to-all-start.1 = ((f32[4,1,256]{2,1,0:T(1,128)}), f32[4,1,256]{2,1,0:T(1,128)S(1)}, u32[]{:S(2)}, u32[]{:S(2)}) async-start(f32[4,1,256]{2,1,0:T(1,128)} %get-tuple-element.40), calls=%async_computation.1 | async-start | bytes 8192 | tf_op jit(solution)/shard_map/all_to_all | solution.py:483
  39.0 6.8 %shard_map.124 = (bf16[3,4,128,88]{3,2,1,0:T(8,128)(2,1)}, bf16[3,4,128,88]{3,2,1,0:T(8,128)(2,1)}, f32[4,4,128,128]{3,2,1,0:T(8,128)}, f32[4,4,128,128]{3,2,1,0...) custom-call(bf16[4,128,1408]{2,1,0:T(8,128)(2,1)S(1)} %get-tuple-element.53.normed.normed_far, ...), custom_call_target="tpu_custom_call" | custom-call | tf_op jit(solution)/shard_map/pallas_call | solution.py:48
  46.8 1.9 %collective-permute-start.6 = (bf16[4,128,1408]{2,1,0:T(8,128)(2,1)S(1)}, bf16[4,128,1408]{2,1,0:T(8,128)(2,1)}, u32[]{:S(2)}, u32[]{:S(2)}) collective-permute-start(bf16[4,128,1408]{2,1,0:T(8,128)(2,1)S(1)} %get-tuple-element.53.normed.normed_far), channel_id=1, source_target_pairs={{0,32},{32,0},{64,96},{96,64},{128,160},{160,128},{192,224},{224,1... | collective-permute-start | bytes 4325384 | tf_op jit(solution)/shard_map/ppermute | solution.py:508
  48.7 2.4 %collective-permute-start.5 = (f32[4,4,128,128]{3,2,1,0:T(8,128)}, f32[4,4,128,128]{3,2,1,0:T(8,128)}, u32[]{:S(2)}, u32[]{:S(2)}) collective-permute-start(f32[4,4,128,128]{3,2,1,0:T(8,128)} %get-tuple-element.52), channel_id=1, source_target_pairs={{0,32},{32,0},{64,96},{96,64},{128,160},{160,128},{192,224},{224,1... | collective-permute-start | bytes 3145736 | tf_op jit(solution)/shard_map/ppermute | solution.py:509
  51.1 10.0 %all_to_all.25.got = f32[16,24,128]{2,1,0:T(8,128)S(1)} all-to-all(f32[16,24,128]{2,1,0:T(8,128)S(1)} %shard_map.125), channel_id=1, replica_groups=mesh['frame'=16,'crop'=4,'dp'=8] {'frame'}, dimensions={0} | all-to-all | bytes 393216 | tf_op jit(solution)/shard_map/all_to_all | solution.py:507
  61.1 2.2 %shard_map.126 = (f32[16,24,128]{2,1,0:T(8,128)}, f32[4,256]{1,0:T(4,128)S(1)}, f32[4,88]{1,0:T(4,128)S(1)}) custom-call(f32[16,24,128]{2,1,0:T(8,128)S(1)} %all_to_all.25.got, bf16[256,2048]{1,0:T(8,128)(2,1)S(1)} %copy-done.1, f32[1,2048]{1,0:T(1,128)S(1)} %bitcast.9), custom_call_target="tpu_custom_call" | custom-call | tf_op jit(solution)/shard_map/pallas_call | solution.py:48
  63.4 6.9 %all-to-all-start.3 = ((f32[16,24,128]{2,1,0:T(8,128)}), f32[16,24,128]{2,1,0:T(8,128)S(1)}, u32[]{:S(2)}, u32[]{:S(2)}) async-start(f32[16,24,128]{2,1,0:T(8,128)} %get-tuple-element.46), calls=%async_computation.3 | async-start | bytes 393216 | tf_op jit(solution)/shard_map/all_to_all | solution.py:523
  70.3 2.3 %collective-permute-start.4 = (bf16[3,4,128,88]{3,2,1,0:T(8,128)(2,1)S(1)}, bf16[3,4,128,88]{3,2,1,0:T(8,128)(2,1)S(1)}, u32[]{:S(2)}, u32[]{:S(2)}) collective-permute-start(bf16[3,4,128,88]{3,2,1,0:T(8,128)(2,1)S(1)} %copy-done.15), channel_id=1, source_target_pairs={{0,32},{32,0},{64,96},{96,64},{128,160},{160,128},{192,224},{224,1... | collective-permute-start | bytes 811016 | tf_op jit(solution)/shard_map/ppermute | solution.py:510
  72.6 3.4 %shard_map.127 = (bf16[1408,512]{1,0:T(8,128)(2,1)}, bf16[1408,512]{1,0:T(8,128)(2,1)}) custom-call(bf16[4,128,1408]{2,1,0:T(8,128)(2,1)} %copy-done, bf16[4,128,1408]{2,1,0:T(8,128)(2,1)} %collective-permute-done.6.normed_oth_far), custom_call_target="tpu_custom_call" | custom-call | tf_op jit(solution)/shard_map/pallas_call | solution.py:48
  76.8 13.0 %shard_map.128 = s16[32,56,256]{2,1,0:T(8,128)(2,1)} custom-call(f32[16,24,128]{2,1,0:T(8,128)S(1)} %all-to-all-done.3.got, f32[4,256]{1,0:T(4,128)S(1)} %get-tuple-element.47.zs, f32[4,88]{1,0:T(4,128)S(1)} %get-tuple-element.48.heads, f32[2,88,256]{2,1,0:T(8,128)S(1)} %copy-done.6, bf16[3,4,128,88]{3,2,1,0:T(8,128)(2,1)} %get-tuple-element.49.own_far, ...), custom_call_target="tpu_custom_call" | custom-call | tf_op jit(solution)/shard_map/pallas_call | solution.py:48
  89.8 14.6 %all-to-all-start.4 = ((s16[32,56,256]{2,1,0:T(8,128)(2,1)}), s16[32,56,256]{2,1,0:T(8,128)(2,1)S(1)}, u32[]{:S(2)}, u32[]{:S(2)}) async-start(s16[32,56,256]{2,1,0:T(8,128)(2,1)} %shard_map.128), calls=%async_computation.4 | async-start | bytes 1835008 | tf_op jit(solution)/shard_map/all_to_all | solution.py:541
  105.2 29.9 %all-to-all-done.4.got = s16[32,56,256]{2,1,0:T(8,128)(2,1)S(1)} async-done(((s16[32,56,256]{2,1,0:T(8,128)(2,1)}), s16[32,56,256]{2,1,0:T(8,128)(2,1)S(1)}, u32[]{:S(2)}, u32[]{:S(2)}) %all-to-all-start.4) | async-done | bytes 917536 | tf_op jit(solution)/shard_map/all_to_all | solution.py:541
  135.1 1.5 %shard_map.129 = (f32[44,264]{1,0:T(8,128)}, f32[44,88]{1,0:T(8,128)}, f32[44,256]{1,0:T(8,128)}) custom-call(s16[32,56,256]{2,1,0:T(8,128)(2,1)S(1)} %all-to-all-done.4.got, bf16[44,256]{1,0:T(8,128)(2,1)S(1)} %constant_dynamic-slice_fusion.bottle), custom_call_target="tpu_custom_call" | custom-call | tf_op jit(solution)/shard_map/pallas_call | solution.py:48
  (41 shorter events, 4.8 us)
Async XLA Ops:
  0.6 0.9 copy-start.7
  2.8 10.2 %copy-start.2 = (bf16[88,1408]{1,0:T(8,128)(2,1)S(1)}, bf16[88,1408]{1,0:T(8,128)(2,1)}, u32[]{:S(2)}) copy-start(bf16[88,1408]{1,0:T(8,128)(2,1)} %s_out_far.1) | copy-start | bytes 743428
  2.8 12.2 %copy-start.10 = (bf16[88,1408]{1,0:T(8,128)(2,1)S(1)}, bf16[88,1408]{1,0:T(8,128)(2,1)}, u32[]{:S(2)}) copy-start(bf16[88,1408]{1,0:T(8,128)(2,1)} %t_out.1) | copy-start | bytes 743428
  2.8 15.7 %copy-start.4 = (bf16[1408,256]{1,0:T(8,128)(2,1)S(1)}, bf16[1408,256]{1,0:T(8,128)(2,1)}, u32[]{:S(2)}) copy-start(bf16[1408,256]{1,0:T(8,128)(2,1)} %s_bot.1) | copy-start | bytes 2162692
  2.8 15.7 %copy-start.8 = (bf16[1,1,64,1408]{3,2,1,0:T(8,128)(2,1)S(1)}, bf16[1,1,64,1408]{3,2,1,0:T(8,128)(2,1)}, u32[]{:S(2)}) copy-start(bf16[1,1,64,1408]{3,2,1,0:T(8,128)(2,1)} %param.10) | copy-start | bytes 540676
  2.8 15.7 %copy-start.13 = (s32[1,4,8]{2,1,0:T(4,128)S(1)}, s32[1,4,8]{2,1,0:T(4,128)}, u32[]{:S(2)}) copy-start(s32[1,4,8]{2,1,0:T(4,128)} %param.11) | copy-start | bytes 388
  2.8 23.2 %all-to-all-start = ((bf16[16,32,1408]{2,1,0:T(8,128)(2,1)}), bf16[16,32,1408]{2,1,0:T(8,128)(2,1)S(1)}, u32[]{:S(2)}, u32[]{:S(2)}) async-start(bf16[16,32,1408]{2,1,0:T(8,128)(2,1)} %shard_map.121), calls=%async_computation | async-start | bytes 2883584 | tf_op jit(solution)/shard_map/all_to_all | solution.py:455
  8.7 14.1 %collective-permute-start = (bf16[264,1408]{1,0:T(8,128)(2,1)}, bf16[264,1408]{1,0:T(8,128)(2,1)}, u32[]{:S(2)}, u32[]{:S(2)}) collective-permute-start(bf16[264,1408]{1,0:T(8,128)(2,1)} %bitcast.11), channel_id=1, source_target_pairs={{0,32},{32,0},{64,96},{96,64},{128,160},{160,128},{192,224},{224,1... | collective-permute-start | bytes 2230280 | tf_op jit(solution)/shard_map/ppermute | solution.py:458
  10.7 28.3 %collective-permute-start.3 = (bf16[264,1408]{1,0:T(8,128)(2,1)}, bf16[264,1408]{1,0:T(8,128)(2,1)}, u32[]{:S(2)}, u32[]{:S(2)}) collective-permute-start(bf16[264,1408]{1,0:T(8,128)(2,1)} %bitcast.13), channel_id=1, source_target_pairs={{0,32},{32,0},{64,96},{96,64},{128,160},{160,128},{192,224},{224,1... | collective-permute-start | bytes 2230280 | tf_op jit(solution)/shard_map/ppermute | solution.py:459
  13.0 4.4 %collective-permute-start.2 = (bf16[88,1408]{1,0:T(8,128)(2,1)S(1)}, bf16[88,1408]{1,0:T(8,128)(2,1)S(1)}, u32[]{:S(2)}, u32[]{:S(2)}) collective-permute-start(bf16[88,1408]{1,0:T(8,128)(2,1)S(1)} %copy-done.2), channel_id=1, source_target_pairs={{0,32},{32,0},{64,96},{96,64},{128,160},{160,128},{192,224},{224,1... | collective-permute-start | bytes 743432 | tf_op jit(solution)/shard_map/ppermute | solution.py:461
  15.0 3.4 %collective-permute-start.1 = (bf16[88,1408]{1,0:T(8,128)(2,1)S(1)}, bf16[88,1408]{1,0:T(8,128)(2,1)S(1)}, u32[]{:S(2)}, u32[]{:S(2)}) collective-permute-start(bf16[88,1408]{1,0:T(8,128)(2,1)S(1)} %copy-done.10), channel_id=1, source_target_pairs={{0,32},{32,0},{64,96},{96,64},{128,160},{160,128},{192,224},{224,1... | collective-permute-start | bytes 743432 | tf_op jit(solution)/shard_map/ppermute | solution.py:460
  17.4 15.3 %copy-start.3 = (bf16[88,1408]{1,0:T(8,128)(2,1)}, bf16[88,1408]{1,0:T(8,128)(2,1)S(1)}, u32[]{:S(2)}) copy-start(bf16[88,1408]{1,0:T(8,128)(2,1)S(1)} %collective-permute-done.2.s_oth.s_oth_far) | copy-start | bytes 743428
  18.5 1.1 copy-start.9
  32.7 14.0 %copy-start = (bf16[4,128,1408]{2,1,0:T(8,128)(2,1)}, bf16[4,128,1408]{2,1,0:T(8,128)(2,1)S(1)}, u32[]{:S(2)}) copy-start(bf16[4,128,1408]{2,1,0:T(8,128)(2,1)S(1)} %get-tuple-element.53.normed.normed_far) | copy-start | bytes 4325380
  32.7 13.9 %all-to-all-start.1 = ((f32[4,1,256]{2,1,0:T(1,128)}), f32[4,1,256]{2,1,0:T(1,128)S(1)}, u32[]{:S(2)}, u32[]{:S(2)}) async-start(f32[4,1,256]{2,1,0:T(1,128)} %get-tuple-element.40), calls=%async_computation.1 | async-start | bytes 8192 | tf_op jit(solution)/shard_map/all_to_all | solution.py:483
  38.9 22.2 %copy-start.1 = (bf16[256,2048]{1,0:T(8,128)(2,1)S(1)}, bf16[256,2048]{1,0:T(8,128)(2,1)}, u32[]{:S(2)}) copy-start(bf16[256,2048]{1,0:T(8,128)(2,1)} %protos.1) | copy-start | bytes 3145732
  38.9 22.2 %copy-start.12 = (f32[2048]{0:T(1024)S(1)}, f32[2048]{0:T(1024)}, u32[]{:S(2)}) copy-start(f32[2048]{0:T(1024)} %param.19) | copy-start | bytes 24580
  45.8 24.5 %copy-start.15 = (bf16[3,4,128,88]{3,2,1,0:T(8,128)(2,1)S(1)}, bf16[3,4,128,88]{3,2,1,0:T(8,128)(2,1)}, u32[]{:S(2)}) copy-start(bf16[3,4,128,88]{3,2,1,0:T(8,128)(2,1)} %get-tuple-element.50) | copy-start | bytes 811012
  46.8 25.9 %collective-permute-start.6 = (bf16[4,128,1408]{2,1,0:T(8,128)(2,1)S(1)}, bf16[4,128,1408]{2,1,0:T(8,128)(2,1)}, u32[]{:S(2)}, u32[]{:S(2)}) collective-permute-start(bf16[4,128,1408]{2,1,0:T(8,128)(2,1)S(1)} %get-tuple-element.53.normed.normed_far), channel_id=1, source_target_pairs={{0,32},{32,0},{64,96},{96,64},{128,160},{160,128},{192,224},{224,1... | collective-permute-start | bytes 4325384 | tf_op jit(solution)/shard_map/ppermute | solution.py:508
  48.7 27.4 %collective-permute-start.5 = (f32[4,4,128,128]{3,2,1,0:T(8,128)}, f32[4,4,128,128]{3,2,1,0:T(8,128)}, u32[]{:S(2)}, u32[]{:S(2)}) collective-permute-start(f32[4,4,128,128]{3,2,1,0:T(8,128)} %get-tuple-element.52), channel_id=1, source_target_pairs={{0,32},{32,0},{64,96},{96,64},{128,160},{160,128},{192,224},{224,1... | collective-permute-start | bytes 3145736 | tf_op jit(solution)/shard_map/ppermute | solution.py:509
  63.4 12.7 %all-to-all-start.3 = ((f32[16,24,128]{2,1,0:T(8,128)}), f32[16,24,128]{2,1,0:T(8,128)S(1)}, u32[]{:S(2)}, u32[]{:S(2)}) async-start(f32[16,24,128]{2,1,0:T(8,128)} %get-tuple-element.46), calls=%async_computation.3 | async-start | bytes 393216 | tf_op jit(solution)/shard_map/all_to_all | solution.py:523
  70.3 6.5 %copy-start.6 = (f32[2,88,256]{2,1,0:T(8,128)S(1)}, f32[2,88,256]{2,1,0:T(8,128)}, u32[]{:S(2)}) copy-start(f32[2,88,256]{2,1,0:T(8,128)} %copy-done.5) | copy-start | bytes 540676
  70.3 5.7 %collective-permute-start.4 = (bf16[3,4,128,88]{3,2,1,0:T(8,128)(2,1)S(1)}, bf16[3,4,128,88]{3,2,1,0:T(8,128)(2,1)S(1)}, u32[]{:S(2)}, u32[]{:S(2)}) collective-permute-start(bf16[3,4,128,88]{3,2,1,0:T(8,128)(2,1)S(1)} %copy-done.15), channel_id=1, source_target_pairs={{0,32},{32,0},{64,96},{96,64},{128,160},{160,128},{192,224},{224,1... | collective-permute-start | bytes 811016 | tf_op jit(solution)/shard_map/ppermute | solution.py:510
  89.8 45.3 %all-to-all-start.4 = ((s16[32,56,256]{2,1,0:T(8,128)(2,1)}), s16[32,56,256]{2,1,0:T(8,128)(2,1)S(1)}, u32[]{:S(2)}, u32[]{:S(2)}) async-start(s16[32,56,256]{2,1,0:T(8,128)(2,1)} %shard_map.128), calls=%async_computation.4 | async-start | bytes 1835008 | tf_op jit(solution)/shard_map/all_to_all | solution.py:541
  (3 other events, 2.1 us)
where the time goes:
time: 137 us
  starting transfers between devices  48.9 us (36%)
  Pallas kernels  36.8 us (27%)
  waiting for transfers between devices  35.1 us (26%)
  blocking collectives  10 us (7%)
  local copies, waits for them, and re-layouts  4.87 us (4%)
    pallas_call x9, Pallas kernels, call(): pl.pallas_call(kernel, out_shape=tuple((pltpu.HBM(shape, dtype) if index...  36.8 us
    all_to_all x1, waiting for transfers between devices, local(): got = lax.all_to_all(sent, ('crop', 'dp'), 0, 0, tiled=True)  29.9 us
    all_to_all x1, starting transfers between devices, local(): got = lax.all_to_all(sent, ('crop', 'dp'), 0, 0, tiled=True)  14.6 us
    all_to_all x1, blocking collectives, local(): got = lax.all_to_all(sent, 'frame', 0, 0, tiled=True)  10 us
    all_to_all x1, starting transfers between devices, local(): got = lax.all_to_all(sent, 'frame', 0, 0, tiled=True)  6.88 us
    all_to_all x1, starting transfers between devices, local(): ztc = lax.all_to_all(zt, 'crop', 0, 0, tiled=True)  6.21 us
    all_to_all x1, starting transfers between devices, local(): mixed = lax.all_to_all(spread, 'frame', 0, 0, tiled=True)  5.84 us
    unnamed x32, local copies, waits for them, and re-layouts  4.11 us
  transfers between devices with their start and end apart: 11, of which 4 were waited for; matrix products, arithmetic and copies ran while one was open for 1% of the time, Pallas kernels for 15%

commit v1 on v0

--- a/solution.py
+++ b/solution.py
@@ -17,6 +17,8 @@
 ROWS = FRAMES * GP
 TILES = 4
 LFRAMES = 8
+QKV = 3 * HS
+PITCH = 272
 CLIPS = 4
 NTOK = 512
 NTEACH = 4096
@@ -102,9 +104,9 @@
     return jnp.where((row % GP) == (col % GP), 0.0, NEG).astype(F32)
 
 
-def split_qkv(flat):
-    rounded = flat.astype(BF16)
-    return rounded[:, :HS], rounded[:, HS : 2 * HS], rounded[:, 2 * HS :]
+def split_qkv(flat, tile, head):
+    rows = flat[tile * ROWS : (tile + 1) * ROWS]
+    return [rows[:, head * PITCH + part * HS : head * PITCH + (part + 1) * HS].astype(BF16) for part in range(3)]
 
 
 def spread_kernel(tok, out):
@@ -125,27 +127,25 @@
     ms[1] = mm(s_oth[...], s_bot[...])
     lane = lax.broadcasted_iota(jnp.int32, (1, ROWS), 1)
     row = lax.broadcasted_iota(jnp.int32, (ROWS, ROWS), 0) // GP
-    down = jnp.zeros((ROWS, ROWS), F32)
+    down = [jnp.zeros((ROWS, ROWS), F32) for _ in range(CLIPS)]
     across = [jnp.zeros((1, ROWS), F32) for _ in range(CLIPS)]
     mine = [jnp.zeros((1, ROWS), F32) for _ in range(CLIPS)]
     for step in range(LFRAMES):
-        shown = jnp.full((1, ROWS), -1, jnp.int32)
         for clip in range(CLIPS):
             index = maps[clip, step]
-            shown = jnp.where(lane == clip, index, shown)
+            down[clip] = down[clip] + jnp.where(row == index, 1.0, 0.0)
             across[clip] = across[clip] + jnp.where(lane // GP == index, 1.0, 0.0)
             mine[clip] = mine[clip] + jnp.where(index == frame[0], 1.0, 0.0)
-        down = down + jnp.where(row == shown, 1.0, 0.0)
-    crow[...] = down
     for clip in range(CLIPS):
+        crow[clip] = down[clip]
         ccol[clip : clip + 1, :] = across[clip]
         frac = mine[clip][:, 0:1] / NTOK
         zlocal[clip : clip + 1, :] = frac * osz
         plocal[clip : clip + 1, :] = frac * total
 
 
-def teacher_kernel(x, w_own_far, w_oth_far, mt_far, otz, normed, zt, w_own, w_oth, mt, sems):
-    copies = begin((w_own_far, w_oth_far, mt_far), (w_own, w_oth, mt), sems)
+def teacher_kernel(x, w_own_far, w_oth_far, mt_far, otz, normed, zt, weights, mt, sems):
+    copies = begin((w_own_far, w_oth_far, mt_far), (weights.at[pl.ds(0, QKV)], weights.at[pl.ds(PITCH, QKV)], mt), sems)
     for group in range(2):
         values = x[:, group * 2 * GP : (group + 1) * 2 * GP, :].astype(F32)
         middle = jnp.mean(values, axis=-1, keepdims=True)
@@ -157,56 +157,63 @@
     mask = same_patch()
     tokens = normed[...].reshape(TILES * ROWS, D)
     total = otz[...]
-    copies[2].wait()
-    for head, weight in enumerate((w_own, w_oth)):
-        copies[head].wait()
-        flat = mm(tokens, weight[...], NT)
-        summed = jnp.zeros((1, HS), F32)
+    for copy in copies:
+        copy.wait()
+    flat = mm(tokens, weights[...], NT)
+    ones = jnp.ones((8, ROWS), BF16)
+    for head in range(2):
+        summed = jnp.zeros((8, HS), F32)
         for tile in range(TILES):
-            query, key, value = split_qkv(flat[tile * ROWS : (tile + 1) * ROWS])
-            scores = mm(query, key, NT) * SCALE + mask
-            scores = jnp.exp(scores - jnp.max(scores, axis=-1, keepdims=True))
-            share = scores / jnp.sum(scores, axis=-1, keepdims=True)
-            att = mm(share.astype(BF16), value)
-            summed = summed + jnp.sum(att, axis=0, keepdims=True)
-        total = total + mmh(summed, mt[head])
+            query, key, value = split_qkv(flat, tile, head)
+            scores = mm(key, query, NT) * SCALE + mask
+            scores = jnp.exp(scores - jnp.max(scores, axis=0, keepdims=True))
+            share = scores / jnp.sum(scores, axis=0, keepdims=True)
+            received = mm(ones, share.astype(BF16), NT)
+            summed = summed + mm3(received, value)
+        total = total + mmh(summed[0:1], mt[head])
     for crop in range(zt.shape[0]):
         zt[crop] = total / NTEACH
 
 
 def clip_shares(scores, count):
     here = jnp.where(count > 0.0, scores, NEG)
-    here = jnp.exp(here - jnp.max(here, axis=-1, keepdims=True))
-    return here / jnp.sum(here * count, axis=-1, keepdims=True)
+    here = jnp.exp(here - jnp.max(here, axis=0, keepdims=True))
+    return here / jnp.sum(here * count, axis=0, keepdims=True)
 
 
 def student_kernel(
     normed, w_own_far, w_oth_far, ms_far, s_out_far, s_oth_far, zlocal, plocal, ccol, crow,
     own_far, oth_far, shares_own_far, shares_oth_far, zs, pooled, heads,
-    w_own, w_oth, ms, s_out, s_oth, sems, own, oth, shares_own, shares_oth, out_sems,
+    weights, ms, s_out, s_oth, sems, own, oth, shares_own, shares_oth, out_sems,
 ):
-    copies = begin((w_own_far, w_oth_far, ms_far, s_out_far, s_oth_far), (w_own, w_oth, ms, s_out, s_oth), sems)
+    copies = begin(
+        (w_own_far, w_oth_far, ms_far, s_out_far, s_oth_far),
+        (weights.at[pl.ds(0, QKV)], weights.at[pl.ds(PITCH, QKV)], ms, s_out, s_oth),
+        sems,
+    )
     mask = same_patch()
     tokens = normed[...].reshape(TILES * ROWS, D)
     leaving = []
-    sides = ((w_own, own, shares_own, own_far, shares_own_far), (w_oth, oth, shares_oth, oth_far, shares_oth_far))
-    for head, (weight, keep, shares, keep_far, shares_far) in enumerate(sides):
-        copies[head].wait()
-        flat = mm(tokens, weight[...], NT)
+    copies[0].wait()
+    copies[1].wait()
+    flat = mm(tokens, weights[...], NT)
+    counts = jnp.concatenate([ccol[...], ccol[...]], axis=0).astype(BF16)
+    sides = ((own, shares_own, own_far, shares_own_far), (oth, shares_oth, oth_far, shares_oth_far))
+    for head, (keep, shares, keep_far, shares_far) in enumerate(sides):
         summed = jnp.zeros((CLIPS, HS), F32)
         for tile in range(TILES):
-            query, key, value = split_qkv(flat[tile * ROWS : (tile + 1) * ROWS])
+            query, key, value = split_qkv(flat, tile, head)
             keep[0, tile] = query
             keep[1, tile] = key
             keep[2, tile] = value
-            scores = mm(query, key, NT) * SCALE + mask
+            scores = mm(key, query, NT) * SCALE + mask
             totals = []
             for clip in range(CLIPS):
-                count = ccol[clip : clip + 1, :]
-                share = clip_shares(scores, count)
-                shares[tile, clip] = share
-                share = share.astype(BF16).astype(F32) * crow[:, clip : clip + 1]
-                totals.append(jnp.sum(share, axis=0, keepdims=True) * count)
+                share = clip_shares(scores, crow[clip])
+                shares[tile, clip, 0:ROWS, :] = share
+                received = mm(counts, share.astype(BF16), NT)[clip : clip + 1]
+                shares[tile, clip, ROWS : ROWS + 1, :] = received
+                totals.append(received * ccol[clip : clip + 1, :])
             summed = summed + mm3(jnp.concatenate(totals, axis=0), value)
         leaving += begin((keep, shares), (keep_far, shares_far), out_sems.at[pl.ds(2 * head, 2)])
         heads[head] = summed / NTOK
@@ -282,8 +289,8 @@
     return jnp.max(jnp.max(x, axis=-1, keepdims=True), axis=0, keepdims=True)
 
 
-def stack3(parts):
-    return jnp.concatenate([piece for part in parts for piece in pieces(part)], axis=0)
+def stack2(parts):
+    return jnp.concatenate([piece for part in parts for piece in pieces(part)[:2]], axis=0)
 
 
 def back_kernel(
@@ -314,43 +321,30 @@
     unit = z_s * inverse
     d_z = (d_unit - unit * jnp.sum(unit * d_unit, axis=-1, keepdims=True)) * inverse
     d_heads = mmh(d_z, ms[0], NT) / NTOK
-    lane = lax.broadcasted_iota(jnp.int32, (ROWS, ROWS), 1)
     for half, (keep, shares) in enumerate(((keep_own, shares_own), (keep_oth, shares_oth))):
         copies[2 * half].wait()
         copies[2 * half + 1].wait()
         for tile in range(TILES):
             d_weights = mm3(d_heads, keep[2, tile], NT).astype(BF16).astype(F32)
-            taken = [
-                jnp.sum(shares[tile, clip].astype(BF16).astype(F32) * crow[:, clip : clip + 1], axis=0, keepdims=True)
-                for clip in range(CLIPS)
-            ]
+            d_weights = d_weights * SCALE
+            taken = [shares[tile, clip, ROWS : ROWS + 1, :] for clip in range(CLIPS)]
             d_down = jnp.transpose(jnp.concatenate([d_weights] + taken, axis=0))
-            inner = jnp.zeros((ROWS, ROWS), F32)
-            grow_q = []
+            grow_q, grow_k = [], []
             for clip in range(CLIPS):
-                share = shares[tile, clip] * ccol[clip : clip + 1, :]
-                d_w = d_weights[clip : clip + 1, :]
-                mean = jnp.sum(share * d_w, axis=-1, keepdims=True)
-                inner = jnp.where(lane == clip, mean, inner)
-                grow_q.append(share * (d_w - mean) * SCALE)
-            inner = jnp.transpose(inner)
-            grow_k = [
-                jnp.transpose(shares[tile, clip])
-                * ccol[clip : clip + 1, :]
-                * (d_down[:, clip : clip + 1] - inner[clip : clip + 1, :])
-                * SCALE
-                for clip in range(CLIPS)
-            ]
-            wide_q = mm(stack3(grow_q), keep[1, tile])
-            wide_k = mm(stack3(grow_k), keep[0, tile])
+                count = ccol[clip : clip + 1, :]
+                share = shares[tile, clip, 0:ROWS, :]
+                d_w = jnp.broadcast_to(d_down[:, clip : clip + 1], (ROWS, ROWS))
+                mean = jnp.sum(share * (crow[clip] * d_w), axis=0, keepdims=True)
+                base = share * (d_w - mean)
+                grow_k.append(base * count)
+                grow_q.append(jnp.transpose(base) * count)
+            wide_q = mm(stack2(grow_q), keep[1, tile])
+            wide_k = mm(stack2(grow_k), keep[0, tile])
             totals = [jnp.zeros((ROWS, HS), F32) for _ in range(3)]
             for clip in range(CLIPS):
-                many = crow[:, clip : clip + 1]
-                first = 3 * clip * ROWS
-                parts = [
-                    wide[first : first + ROWS] + (wide[first + ROWS : first + 2 * ROWS] + wide[first + 2 * ROWS : first + 3 * ROWS])
-                    for wide in (wide_q, wide_k)
-                ]
+                many = crow[clip, :, 0:HS]
+                first = 2 * clip * ROWS
+                parts = [wide[first : first + ROWS] + wide[first + ROWS : first + 2 * ROWS] for wide in (wide_q, wide_k)]
                 parts.append(d_down[:, CLIPS + clip : CLIPS + clip + 1] * d_heads[clip : clip + 1, :])
                 totals = [total + many * part.astype(BF16).astype(F32) for total, part in zip(totals, parts)]
             packed = jnp.concatenate(totals, axis=1)
@@ -468,7 +462,7 @@
             ((CLIPS, BOTTLE), F32),
             ((CLIPS, D), F32),
             ((CLIPS, ROWS), F32),
-            ((ROWS, ROWS), F32),
+            ((CLIPS, ROWS, ROWS), F32),
         ],
         frame_map[0], frame.astype(jnp.int32).reshape(1),
         tokens, teacher_out, t_out_oth, student_out, s_out_oth, teacher_bottle, student_bottle,
@@ -478,11 +472,12 @@
         teacher_kernel,
         [((TILES, ROWS, D), BF16), ((crops, 1, BOTTLE), F32)],
         mixed, t_own, t_oth, mt, otz,
-        hbm_in=(1, 2, 3), scratch=room(t_own, t_oth, mt),
+        hbm_in=(1, 2, 3),
+        scratch=[pltpu.VMEM((2 * PITCH, D), BF16), pltpu.VMEM(mt.shape, F32), pltpu.SemaphoreType.DMA((3,))],
     )
     ztc = lax.all_to_all(zt, "crop", 0, 0, tiled=True)
     keep = jax.ShapeDtypeStruct((3, TILES, ROWS, HS), BF16)
-    table = jax.ShapeDtypeStruct((TILES, CLIPS, ROWS, ROWS), F32)
+    table = jax.ShapeDtypeStruct((TILES, CLIPS, ROWS + 8, ROWS), F32)
     own, oth, shares_own, shares_oth, zs, pooled, heads = call(
         student_kernel,
         [
@@ -496,7 +491,10 @@
         ],
         normed, s_own, s_oth, ms, student_out, s_out_oth, zlocal, plocal, ccol, crow,
         hbm_in=(1, 2, 3, 4, 5), hbm_out=(0, 1, 2, 3), limit=20,
-        scratch=room(s_own, s_oth, ms, student_out, s_out_oth) + room(keep, keep, table, table),
+        scratch=[pltpu.VMEM((2 * PITCH, D), BF16)]
+        + room(ms, student_out, s_out_oth)[:-1]
+        + [pltpu.SemaphoreType.DMA((5,))]
+        + room(keep, keep, table, table),
     )
     (sent,) = call(
         message_kernel,

time: 137 us -> 135 us (0.985)
  Pallas kernels: 36.8 us -> 34.8 us
  local copies, waits for them, and re-layouts: 4.87 us -> 6.53 us
  waiting for transfers between devices: 35.1 us -> 33.6 us
    pallas_call x9, Pallas kernels: 36.8 us -> 34.8 us  [call(): pl.pallas_call(kernel, out_shape=tuple((pltpu.HBM(shape, dtype) if index...]
    all_to_all x1, waiting for transfers between devices: 3.24 us -> 1.44 us  [local(): mixed = lax.all_to_all(spread, 'frame', 0, 0, tiled=True)]
    unnamed x32 -> x36, local copies, waits for them, and re-layouts: 4.11 us -> 5.76 us
where the time goes in v1:
time: 135 us
  starting transfers between devices  48.6 us (36%)
  Pallas kernels  34.8 us (26%)
  waiting for transfers between devices  33.6 us (25%)
  blocking collectives  10 us (7%)
  local copies, waits for them, and re-layouts  6.53 us (5%)
    pallas_call x9, Pallas kernels, call(): pl.pallas_call(kernel, out_shape=tuple((pltpu.HBM(shape, dtype) if index...  34.8 us
    all_to_all x1, waiting for transfers between devices, local(): got = lax.all_to_all(sent, ('crop', 'dp'), 0, 0, tiled=True)  29.9 us
    all_to_all x1, starting transfers between devices, local(): got = lax.all_to_all(sent, ('crop', 'dp'), 0, 0, tiled=True)  14.4 us
    all_to_all x1, blocking collectives, local(): got = lax.all_to_all(sent, 'frame', 0, 0, tiled=True)  10 us
    all_to_all x1, starting transfers between devices, local(): got = lax.all_to_all(sent, 'frame', 0, 0, tiled=True)  6.88 us
    all_to_all x1, starting transfers between devices, local(): ztc = lax.all_to_all(zt, 'crop', 0, 0, tiled=True)  6.21 us
    all_to_all x1, starting transfers between devices, local(): mixed = lax.all_to_all(spread, 'frame', 0, 0, tiled=True)  5.84 us
    unnamed x36, local copies, waits for them, and re-layouts  5.76 us
  transfers between devices with their start and end apart: 11, of which 4 were waited for; matrix products, arithmetic and copies ran while one was open for 1% of the time, Pallas kernels for 15%

profile of v1, /device:TPU:78, one launch (start us, length us, event | category | flops | bytes accessed | tf_op | source)
XLA Modules:
  0.0 134.5 jit_solution(6843470926820014013)
XLA Ops:
  1.6 1.3 shard_map.121
  2.8 5.8 %all-to-all-start = ((bf16[16,32,1408]{2,1,0:T(8,128)(2,1)}), bf16[16,32,1408]{2,1,0:T(8,128)(2,1)S(1)}, u32[]{:S(2)}, u32[]{:S(2)}) async-start(bf16[16,32,1408]{2,1,0:T(8,128)(2,1)} %shard_map.121), calls=%async_computation | async-start | bytes 2883584 | tf_op jit(solution)/shard_map/all_to_all | solution.py:449
  8.7 2.0 %collective-permute-start = (bf16[264,1408]{1,0:T(8,128)(2,1)}, bf16[264,1408]{1,0:T(8,128)(2,1)}, u32[]{:S(2)}, u32[]{:S(2)}) collective-permute-start(bf16[264,1408]{1,0:T(8,128)(2,1)} %bitcast.11), channel_id=1, source_target_pairs={{0,32},{32,0},{64,96},{96,64},{128,160},{160,128},{192,224},{224,1... | collective-permute-start | bytes 2230280 | tf_op jit(solution)/shard_map/ppermute | solution.py:452
  10.7 2.3 %collective-permute-start.3 = (bf16[264,1408]{1,0:T(8,128)(2,1)}, bf16[264,1408]{1,0:T(8,128)(2,1)}, u32[]{:S(2)}, u32[]{:S(2)}) collective-permute-start(bf16[264,1408]{1,0:T(8,128)(2,1)} %bitcast.13), channel_id=1, source_target_pairs={{0,32},{32,0},{64,96},{96,64},{128,160},{160,128},{192,224},{224,1... | collective-permute-start | bytes 2230280 | tf_op jit(solution)/shard_map/ppermute | solution.py:453
  13.0 2.0 %collective-permute-start.2 = (bf16[88,1408]{1,0:T(8,128)(2,1)S(1)}, bf16[88,1408]{1,0:T(8,128)(2,1)S(1)}, u32[]{:S(2)}, u32[]{:S(2)}) collective-permute-start(bf16[88,1408]{1,0:T(8,128)(2,1)S(1)} %copy-done.2), channel_id=1, source_target_pairs={{0,32},{32,0},{64,96},{96,64},{128,160},{160,128},{192,224},{224,1... | collective-permute-start | bytes 743432 | tf_op jit(solution)/shard_map/ppermute | solution.py:455
  15.1 2.3 %collective-permute-start.1 = (bf16[88,1408]{1,0:T(8,128)(2,1)S(1)}, bf16[88,1408]{1,0:T(8,128)(2,1)S(1)}, u32[]{:S(2)}, u32[]{:S(2)}) collective-permute-start(bf16[88,1408]{1,0:T(8,128)(2,1)S(1)} %copy-done.10), channel_id=1, source_target_pairs={{0,32},{32,0},{64,96},{96,64},{128,160},{160,128},{192,224},{224,1... | collective-permute-start | bytes 743432 | tf_op jit(solution)/shard_map/ppermute | solution.py:454
  19.2 1.1 copy-done.7
  21.3 1.9 %shard_map.122 = (f32[2,88,256]{2,1,0:T(8,128)S(1)}, f32[2,88,256]{2,1,0:T(8,128)S(1)}, f32[1,256]{1,0:T(1,128)S(1)}, f32[4,256]{1,0:T(4,128)S(1)}, f32[4,1408]{...) custom-call(s32[4,8]{1,0:T(4,128)S(1)} %bitcast.10, s32[1]{0:T(128)} %bitcast.frame, ...), custom_call_target="tpu_custom_call" | custom-call | tf_op jit(solution)/shard_map/pallas_call | solution.py:50
  24.5 1.4 %all-to-all-done.x = bf16[16,32,1408]{2,1,0:T(8,128)(2,1)S(1)} async-done(((bf16[16,32,1408]{2,1,0:T(8,128)(2,1)}), bf16[16,32,1408]{2,1,0:T(8,128)(2,1)S(1)}, u32[]{:S(2)}, u32[]{:S(2)}) %all-to-all-start) | async-done | bytes 1441824 | tf_op jit(solution)/shard_map/all_to_all | solution.py:449
  26.0 5.7 %shard_map.123 = (bf16[4,128,1408]{2,1,0:T(8,128)(2,1)S(1)}, f32[4,1,256]{2,1,0:T(1,128)}) custom-call(bf16[16,32,1408]{2,1,0:T(8,128)(2,1)S(1)} %all-to-all-done.x, bf16[264,1408]{1,0:T(8,128)(2,1)} %bitcast.12, bf16[264,1408]{1,0:T(8,128)(2,1)} %collective-permute-done.w_oth_far, f32[2,88,256]{2,1,0:T(8,128)} %copy-done.13, f32[1,256]{1,0:T(1,128)S(1)} %get-tuple-element.32.otz), custom_call_target="tpu_custom_call" | custom-call | tf_op jit(solution)/shard_map/pallas_call | solution.py:50
  31.8 6.2 %all-to-all-start.1 = ((f32[4,1,256]{2,1,0:T(1,128)}), f32[4,1,256]{2,1,0:T(1,128)S(1)}, u32[]{:S(2)}, u32[]{:S(2)}) async-start(f32[4,1,256]{2,1,0:T(1,128)} %get-tuple-element.40), calls=%async_computation.1 | async-start | bytes 8192 | tf_op jit(solution)/shard_map/all_to_all | solution.py:478
  38.0 6.5 %shard_map.124 = (bf16[3,4,128,88]{3,2,1,0:T(8,128)(2,1)}, bf16[3,4,128,88]{3,2,1,0:T(8,128)(2,1)}, f32[4,4,136,128]{3,2,1,0:T(8,128)}, f32[4,4,136,128]{3,2,1,0...) custom-call(bf16[4,128,1408]{2,1,0:T(8,128)(2,1)S(1)} %get-tuple-element.53.normed.normed_far, ...), custom_call_target="tpu_custom_call" | custom-call | tf_op jit(solution)/shard_map/pallas_call | solution.py:50
  44.5 1.1 all-to-all-done.1.ztc
  45.8 1.9 %collective-permute-start.6 = (bf16[4,128,1408]{2,1,0:T(8,128)(2,1)S(1)}, bf16[4,128,1408]{2,1,0:T(8,128)(2,1)}, u32[]{:S(2)}, u32[]{:S(2)}) collective-permute-start(bf16[4,128,1408]{2,1,0:T(8,128)(2,1)S(1)} %get-tuple-element.53.normed.normed_far), channel_id=1, source_target_pairs={{0,32},{32,0},{64,96},{96,64},{128,160},{160,128},{192,224},{224,1... | collective-permute-start | bytes 4325384 | tf_op jit(solution)/shard_map/ppermute | solution.py:506
  47.7 2.4 %collective-permute-start.5 = (f32[4,4,136,128]{3,2,1,0:T(8,128)}, f32[4,4,136,128]{3,2,1,0:T(8,128)}, u32[]{:S(2)}, u32[]{:S(2)}) collective-permute-start(f32[4,4,136,128]{3,2,1,0:T(8,128)} %get-tuple-element.52), channel_id=1, source_target_pairs={{0,32},{32,0},{64,96},{96,64},{128,160},{160,128},{192,224},{224,1... | collective-permute-start | bytes 3342344 | tf_op jit(solution)/shard_map/ppermute | solution.py:507
  50.1 10.0 %all_to_all.25.got = f32[16,24,128]{2,1,0:T(8,128)S(1)} all-to-all(f32[16,24,128]{2,1,0:T(8,128)S(1)} %shard_map.125), channel_id=1, replica_groups=mesh['frame'=16,'crop'=4,'dp'=8] {'frame'}, dimensions={0} | all-to-all | bytes 393216 | tf_op jit(solution)/shard_map/all_to_all | solution.py:505
  60.1 2.2 %shard_map.126 = (f32[16,24,128]{2,1,0:T(8,128)}, f32[4,256]{1,0:T(4,128)S(1)}, f32[4,88]{1,0:T(4,128)S(1)}) custom-call(f32[16,24,128]{2,1,0:T(8,128)S(1)} %all_to_all.25.got, bf16[256,2048]{1,0:T(8,128)(2,1)S(1)} %copy-done.1, f32[1,2048]{1,0:T(1,128)S(1)} %bitcast.9), custom_call_target="tpu_custom_call" | custom-call | tf_op jit(solution)/shard_map/pallas_call | solution.py:50
  62.4 6.9 %all-to-all-start.3 = ((f32[16,24,128]{2,1,0:T(8,128)}), f32[16,24,128]{2,1,0:T(8,128)S(1)}, u32[]{:S(2)}, u32[]{:S(2)}) async-start(f32[16,24,128]{2,1,0:T(8,128)} %get-tuple-element.46), calls=%async_computation.3 | async-start | bytes 393216 | tf_op jit(solution)/shard_map/all_to_all | solution.py:521
  69.3 2.3 %collective-permute-start.4 = (bf16[3,4,128,88]{3,2,1,0:T(8,128)(2,1)S(1)}, bf16[3,4,128,88]{3,2,1,0:T(8,128)(2,1)S(1)}, u32[]{:S(2)}, u32[]{:S(2)}) collective-permute-start(bf16[3,4,128,88]{3,2,1,0:T(8,128)(2,1)S(1)} %copy-done.17), channel_id=1, source_target_pairs={{0,32},{32,0},{64,96},{96,64},{128,160},{160,128},{192,224},{224,1... | collective-permute-start | bytes 811016 | tf_op jit(solution)/shard_map/ppermute | solution.py:508
  71.6 3.4 %shard_map.127 = (bf16[1408,512]{1,0:T(8,128)(2,1)}, bf16[1408,512]{1,0:T(8,128)(2,1)}) custom-call(bf16[4,128,1408]{2,1,0:T(8,128)(2,1)} %copy-done, bf16[4,128,1408]{2,1,0:T(8,128)(2,1)} %collective-permute-done.6.normed_oth_far), custom_call_target="tpu_custom_call" | custom-call | tf_op jit(solution)/shard_map/pallas_call | solution.py:50
  75.8 12.1 %shard_map.128 = s16[32,56,256]{2,1,0:T(8,128)(2,1)} custom-call(f32[16,24,128]{2,1,0:T(8,128)S(1)} %all-to-all-done.3.got, f32[4,256]{1,0:T(4,128)S(1)} %get-tuple-element.47.zs, f32[4,88]{1,0:T(4,128)S(1)} %get-tuple-element.48.heads, f32[2,88,256]{2,1,0:T(8,128)S(1)} %copy-done.9, bf16[3,4,128,88]{3,2,1,0:T(8,128)(2,1)} %get-tuple-element.49.own_far, ...), custom_call_target="tpu_custom_call" | custom-call | tf_op jit(solution)/shard_map/pallas_call | solution.py:50
  87.9 14.4 %all-to-all-start.4 = ((s16[32,56,256]{2,1,0:T(8,128)(2,1)}), s16[32,56,256]{2,1,0:T(8,128)(2,1)S(1)}, u32[]{:S(2)}, u32[]{:S(2)}) async-start(s16[32,56,256]{2,1,0:T(8,128)(2,1)} %shard_map.128), calls=%async_computation.4 | async-start | bytes 1835008 | tf_op jit(solution)/shard_map/all_to_all | solution.py:539
  103.1 29.9 %all-to-all-done.4.got = s16[32,56,256]{2,1,0:T(8,128)(2,1)S(1)} async-done(((s16[32,56,256]{2,1,0:T(8,128)(2,1)}), s16[32,56,256]{2,1,0:T(8,128)(2,1)S(1)}, u32[]{:S(2)}, u32[]{:S(2)}) %all-to-all-start.4) | async-done | bytes 917536 | tf_op jit(solution)/shard_map/all_to_all | solution.py:539
  133.0 1.5 %shard_map.129 = (f32[44,264]{1,0:T(8,128)}, f32[44,88]{1,0:T(8,128)}, f32[44,256]{1,0:T(8,128)}) custom-call(s16[32,56,256]{2,1,0:T(8,128)(2,1)S(1)} %all-to-all-done.4.got, bf16[44,256]{1,0:T(8,128)(2,1)S(1)} %constant_dynamic-slice_fusion.bottle), custom_call_target="tpu_custom_call" | custom-call | tf_op jit(solution)/shard_map/pallas_call | solution.py:50
  (45 shorter events, 6.6 us)
Async XLA Ops:
  2.8 10.2 %copy-start.2 = (bf16[88,1408]{1,0:T(8,128)(2,1)S(1)}, bf16[88,1408]{1,0:T(8,128)(2,1)}, u32[]{:S(2)}) copy-start(bf16[88,1408]{1,0:T(8,128)(2,1)} %s_out_far.1) | copy-start | bytes 743428
  2.8 12.2 %copy-start.10 = (bf16[88,1408]{1,0:T(8,128)(2,1)S(1)}, bf16[88,1408]{1,0:T(8,128)(2,1)}, u32[]{:S(2)}) copy-start(bf16[88,1408]{1,0:T(8,128)(2,1)} %t_out.1) | copy-start | bytes 743428
  2.8 16.4 %copy-start.4 = (bf16[1408,256]{1,0:T(8,128)(2,1)S(1)}, bf16[1408,256]{1,0:T(8,128)(2,1)}, u32[]{:S(2)}) copy-start(bf16[1408,256]{1,0:T(8,128)(2,1)} %s_bot.1) | copy-start | bytes 2162692
  2.8 16.4 %copy-start.6 = (bf16[1,1,64,1408]{3,2,1,0:T(8,128)(2,1)S(1)}, bf16[1,1,64,1408]{3,2,1,0:T(8,128)(2,1)}, u32[]{:S(2)}) copy-start(bf16[1,1,64,1408]{3,2,1,0:T(8,128)(2,1)} %param.10) | copy-start | bytes 540676
  2.8 16.4 %copy-start.15 = (s32[1,4,8]{2,1,0:T(4,128)S(1)}, s32[1,4,8]{2,1,0:T(4,128)}, u32[]{:S(2)}) copy-start(s32[1,4,8]{2,1,0:T(4,128)} %param.11) | copy-start | bytes 388
  2.8 23.2 %all-to-all-start = ((bf16[16,32,1408]{2,1,0:T(8,128)(2,1)}), bf16[16,32,1408]{2,1,0:T(8,128)(2,1)S(1)}, u32[]{:S(2)}, u32[]{:S(2)}) async-start(bf16[16,32,1408]{2,1,0:T(8,128)(2,1)} %shard_map.121), calls=%async_computation | async-start | bytes 2883584 | tf_op jit(solution)/shard_map/all_to_all | solution.py:449
  8.7 15.9 %collective-permute-start = (bf16[264,1408]{1,0:T(8,128)(2,1)}, bf16[264,1408]{1,0:T(8,128)(2,1)}, u32[]{:S(2)}, u32[]{:S(2)}) collective-permute-start(bf16[264,1408]{1,0:T(8,128)(2,1)} %bitcast.11), channel_id=1, source_target_pairs={{0,32},{32,0},{64,96},{96,64},{128,160},{160,128},{192,224},{224,1... | collective-permute-start | bytes 2230280 | tf_op jit(solution)/shard_map/ppermute | solution.py:452
  10.7 27.3 %collective-permute-start.3 = (bf16[264,1408]{1,0:T(8,128)(2,1)}, bf16[264,1408]{1,0:T(8,128)(2,1)}, u32[]{:S(2)}, u32[]{:S(2)}) collective-permute-start(bf16[264,1408]{1,0:T(8,128)(2,1)} %bitcast.13), channel_id=1, source_target_pairs={{0,32},{32,0},{64,96},{96,64},{128,160},{160,128},{192,224},{224,1... | collective-permute-start | bytes 2230280 | tf_op jit(solution)/shard_map/ppermute | solution.py:453
  13.0 4.4 %collective-permute-start.2 = (bf16[88,1408]{1,0:T(8,128)(2,1)S(1)}, bf16[88,1408]{1,0:T(8,128)(2,1)S(1)}, u32[]{:S(2)}, u32[]{:S(2)}) collective-permute-start(bf16[88,1408]{1,0:T(8,128)(2,1)S(1)} %copy-done.2), channel_id=1, source_target_pairs={{0,32},{32,0},{64,96},{96,64},{128,160},{160,128},{192,224},{224,1... | collective-permute-start | bytes 743432 | tf_op jit(solution)/shard_map/ppermute | solution.py:455
  15.1 3.4 %collective-permute-start.1 = (bf16[88,1408]{1,0:T(8,128)(2,1)S(1)}, bf16[88,1408]{1,0:T(8,128)(2,1)S(1)}, u32[]{:S(2)}, u32[]{:S(2)}) collective-permute-start(bf16[88,1408]{1,0:T(8,128)(2,1)S(1)} %copy-done.10), channel_id=1, source_target_pairs={{0,32},{32,0},{64,96},{96,64},{128,160},{160,128},{192,224},{224,1... | collective-permute-start | bytes 743432 | tf_op jit(solution)/shard_map/ppermute | solution.py:454
  17.4 8.6 %copy-start.3 = (bf16[88,1408]{1,0:T(8,128)(2,1)}, bf16[88,1408]{1,0:T(8,128)(2,1)S(1)}, u32[]{:S(2)}) copy-start(bf16[88,1408]{1,0:T(8,128)(2,1)S(1)} %collective-permute-done.2.s_oth.s_oth_far) | copy-start | bytes 743428
  19.2 1.1 copy-start.7
  20.3 0.9 copy-start.12
  31.7 14.0 %copy-start = (bf16[4,128,1408]{2,1,0:T(8,128)(2,1)}, bf16[4,128,1408]{2,1,0:T(8,128)(2,1)S(1)}, u32[]{:S(2)}) copy-start(bf16[4,128,1408]{2,1,0:T(8,128)(2,1)S(1)} %get-tuple-element.53.normed.normed_far) | copy-start | bytes 4325380
  31.8 13.9 %all-to-all-start.1 = ((f32[4,1,256]{2,1,0:T(1,128)}), f32[4,1,256]{2,1,0:T(1,128)S(1)}, u32[]{:S(2)}, u32[]{:S(2)}) async-start(f32[4,1,256]{2,1,0:T(1,128)} %get-tuple-element.40), calls=%async_computation.1 | async-start | bytes 8192 | tf_op jit(solution)/shard_map/all_to_all | solution.py:478
  38.0 22.2 %copy-start.1 = (bf16[256,2048]{1,0:T(8,128)(2,1)S(1)}, bf16[256,2048]{1,0:T(8,128)(2,1)}, u32[]{:S(2)}) copy-start(bf16[256,2048]{1,0:T(8,128)(2,1)} %protos.1) | copy-start | bytes 3145732
  38.0 22.2 %copy-start.14 = (f32[2048]{0:T(1024)S(1)}, f32[2048]{0:T(1024)}, u32[]{:S(2)}) copy-start(f32[2048]{0:T(1024)} %param.19) | copy-start | bytes 24580
  44.5 24.7 %copy-start.17 = (bf16[3,4,128,88]{3,2,1,0:T(8,128)(2,1)S(1)}, bf16[3,4,128,88]{3,2,1,0:T(8,128)(2,1)}, u32[]{:S(2)}) copy-start(bf16[3,4,128,88]{3,2,1,0:T(8,128)(2,1)} %get-tuple-element.50) | copy-start | bytes 811012
  45.8 25.8 %collective-permute-start.6 = (bf16[4,128,1408]{2,1,0:T(8,128)(2,1)S(1)}, bf16[4,128,1408]{2,1,0:T(8,128)(2,1)}, u32[]{:S(2)}, u32[]{:S(2)}) collective-permute-start(bf16[4,128,1408]{2,1,0:T(8,128)(2,1)S(1)} %get-tuple-element.53.normed.normed_far), channel_id=1, source_target_pairs={{0,32},{32,0},{64,96},{96,64},{128,160},{160,128},{192,224},{224,1... | collective-permute-start | bytes 4325384 | tf_op jit(solution)/shard_map/ppermute | solution.py:506
  47.7 27.4 %collective-permute-start.5 = (f32[4,4,136,128]{3,2,1,0:T(8,128)}, f32[4,4,136,128]{3,2,1,0:T(8,128)}, u32[]{:S(2)}, u32[]{:S(2)}) collective-permute-start(f32[4,4,136,128]{3,2,1,0:T(8,128)} %get-tuple-element.52), channel_id=1, source_target_pairs={{0,32},{32,0},{64,96},{96,64},{128,160},{160,128},{192,224},{224,1... | collective-permute-start | bytes 3342344 | tf_op jit(solution)/shard_map/ppermute | solution.py:507
  62.4 12.7 %all-to-all-start.3 = ((f32[16,24,128]{2,1,0:T(8,128)}), f32[16,24,128]{2,1,0:T(8,128)S(1)}, u32[]{:S(2)}, u32[]{:S(2)}) async-start(f32[16,24,128]{2,1,0:T(8,128)} %get-tuple-element.46), calls=%async_computation.3 | async-start | bytes 393216 | tf_op jit(solution)/shard_map/all_to_all | solution.py:521
  69.3 6.5 %copy-start.9 = (f32[2,88,256]{2,1,0:T(8,128)S(1)}, f32[2,88,256]{2,1,0:T(8,128)}, u32[]{:S(2)}) copy-start(f32[2,88,256]{2,1,0:T(8,128)} %copy-done.8) | copy-start | bytes 540676
  69.3 5.8 %collective-permute-start.4 = (bf16[3,4,128,88]{3,2,1,0:T(8,128)(2,1)S(1)}, bf16[3,4,128,88]{3,2,1,0:T(8,128)(2,1)S(1)}, u32[]{:S(2)}, u32[]{:S(2)}) collective-permute-start(bf16[3,4,128,88]{3,2,1,0:T(8,128)(2,1)S(1)} %copy-done.17), channel_id=1, source_target_pairs={{0,32},{32,0},{64,96},{96,64},{128,160},{160,128},{192,224},{224,1... | collective-permute-start | bytes 811016 | tf_op jit(solution)/shard_map/ppermute | solution.py:508
  87.9 45.1 %all-to-all-start.4 = ((s16[32,56,256]{2,1,0:T(8,128)(2,1)}), s16[32,56,256]{2,1,0:T(8,128)(2,1)S(1)}, u32[]{:S(2)}, u32[]{:S(2)}) async-start(s16[32,56,256]{2,1,0:T(8,128)(2,1)} %shard_map.128), calls=%async_computation.4 | async-start | bytes 1835008 | tf_op jit(solution)/shard_map/all_to_all | solution.py:539
  (5 other events, 3.7 us)

commit v2 on v1

--- a/solution.py
+++ b/solution.py
@@ -40,8 +40,10 @@
 TN = (((0,), (0,)), ((), ()))
 
 
-def call(kernel, outs, *args, scratch=(), smem=0, hbm_in=(), hbm_out=(), limit=16):
+def call(kernel, outs, *args, scratch=(), smem=0, hbm_in=(), hbm_out=(), any_in=(), limit=16):
     def space(index, in_hbm):
+        if in_hbm is hbm_in and index in any_in:
+            return pl.BlockSpec(memory_space=pl.ANY)
         return pl.BlockSpec(memory_space=pltpu.HBM if index in in_hbm else pltpu.VMEM)
 
     spec = [pl.BlockSpec(memory_space=pltpu.SMEM)] * smem
@@ -225,15 +227,10 @@
         copy.wait()
 
 
-def flip_kernel(normed_far, normed_oth_far, out_own_far, out_oth_far, half, half_oth, sems, out_own, out_oth, out_sems):
-    copies = begin((normed_far, normed_oth_far), (half, half_oth), sems)
-    leaving = []
-    for index, (held, out, far) in enumerate(((half, out_own, out_own_far), (half_oth, out_oth, out_oth_far))):
-        copies[index].wait()
-        out[...] = jnp.transpose(held[...].reshape(TILES * ROWS, D))
-        leaving += begin((out,), (far,), out_sems.at[pl.ds(index, 1)])
-    for copy in leaving:
-        copy.wait()
+def flip_kernel(normed, out_far, out, sems):
+    out[...] = jnp.transpose(normed[...].reshape(TILES * ROWS, D))
+    (copy,) = begin((out,), (out_far,), sems)
+    copy.wait()
 
 
 def message_kernel(frame, zs, ztc, pooled, heads, out):
@@ -356,9 +353,14 @@
             rhs[rows, 512:528] = jnp.concatenate([first[:, 256:264], second[:, 256:264]], axis=1)
     copies[4].wait()
     copies[5].wait()
-    wide = mm(flip[...], rhs[...])
-    main = wide[:, 0:256] + wide[:, 256:512]
-    thin = jnp.transpose(wide[:, 512:520] + wide[:, 520:528])
+    strip = D // 4
+    thin = []
+    for part in range(4):
+        wide = mm(flip[part * strip : (part + 1) * strip, :], rhs[...])
+        grad[part * strip : (part + 1) * strip, :] = wide[:, 0:256] + wide[:, 256:512]
+        thin.append(wide[:, 512:520] + wide[:, 520:528])
+    thin = jnp.transpose(jnp.concatenate(thin, axis=0))
+    main = grad[...]
     code = code_of(jnp.max(jnp.abs(main), axis=0, keepdims=True))
     grad[...] = jnp.round(main * (32000.0 / scale_of(code)))
     code_thin = code_of(jnp.max(jnp.abs(thin), axis=-1, keepdims=True))
@@ -503,16 +505,16 @@
     )
     sent, leaving = lax.optimization_barrier((sent, (normed, oth, shares_oth)))
     got = lax.all_to_all(sent, "frame", 0, 0, tiled=True)
-    normed_oth = lax.ppermute(leaving[0], "frame", swap)
+    flat = jax.ShapeDtypeStruct((D, TILES * ROWS), BF16)
+    (flipped,) = call(
+        flip_kernel,
+        [(flat.shape, BF16)],
+        leaving[0],
+        hbm_out=(0,), scratch=[pltpu.VMEM(flat.shape, BF16), pltpu.SemaphoreType.DMA((1,))],
+    )
+    flipped_oth = lax.ppermute(flipped, "frame", swap)
     shares_got = lax.ppermute(leaving[2], "frame", swap)
     kept_oth = lax.ppermute(leaving[1], "frame", swap)
-    flat = jax.ShapeDtypeStruct((D, TILES * ROWS), BF16)
-    flips = call(
-        flip_kernel,
-        [(flat.shape, BF16), (flat.shape, BF16)],
-        normed, normed_oth,
-        hbm_in=(0, 1), hbm_out=(0, 1), scratch=room(normed, normed_oth) + room(flat, flat),
-    )
     sent, z_s, my_heads = call(
         logits_kernel,
         [((FRAMES, MSG, 128), F32), ((CLIPS, BOTTLE), F32), ((CLIPS, HS), F32)],
@@ -522,8 +524,8 @@
     (sent,) = call(
         functools.partial(back_kernel, peers),
         [((peers, QROWS, 256), jnp.int16)],
-        got, z_s, my_heads, ms, own, kept_oth, shares_own, shares_got, ccol, crow, flips[0], flips[1],
-        hbm_in=(4, 5, 6, 7, 10, 11), hbm_out=(0,), limit=30,
+        got, z_s, my_heads, ms, own, kept_oth, shares_own, shares_got, ccol, crow, flipped, flipped_oth,
+        hbm_in=(4, 6, 10, 11), any_in=(5, 7), hbm_out=(0,), limit=30,
         scratch=room(own, shares_own, kept_oth, shares_got)[:-1]
         + [
             pltpu.VMEM((D, 2 * TILES * ROWS), BF16),

time: 135 us -> 134 us (level)
  the two profiles are of different devices: /device:TPU:78 before, /device:TPU:80 now
where the time goes in v2:
time: 134 us; the launch traced here: 133 us
  starting transfers between devices  46.1 us (34%)
  waiting for transfers between devices  37.6 us (28%)
  Pallas kernels  32.6 us (24%)
  blocking collectives  9.92 us (7%)
  local copies, waits for them, and re-layouts  5.87 us (4%)
    pallas_call x9, Pallas kernels, call(): pl.pallas_call(kernel, out_shape=tuple((pltpu.HBM(shape, dtype) if index...  32.6 us
    all_to_all x1, waiting for transfers between devices, local(): got = lax.all_to_all(sent, ('crop', 'dp'), 0, 0, tiled=True)  26.8 us
    all_to_all x1, starting transfers between devices, local(): got = lax.all_to_all(sent, ('crop', 'dp'), 0, 0, tiled=True)  15 us
    all_to_all x1, blocking collectives, local(): got = lax.all_to_all(sent, 'frame', 0, 0, tiled=True)  9.92 us
    all_to_all x1, starting transfers between devices, local(): ztc = lax.all_to_all(zt, 'crop', 0, 0, tiled=True)  6.53 us
    all_to_all x1, starting transfers between devices, local(): mixed = lax.all_to_all(spread, 'frame', 0, 0, tiled=True)  5.56 us
    all_to_all x1, waiting for transfers between devices, local(): mixed = lax.all_to_all(spread, 'frame', 0, 0, tiled=True)  5.25 us
    unnamed x32, local copies, waits for them, and re-layouts  5.11 us
  transfers between devices with their start and end apart: 11, of which 5 were waited for; matrix products, arithmetic and copies ran while one was open for 1% of the time, Pallas kernels for 12%

profile of v2, /device:TPU:80, one launch (start us, length us, event | category | flops | bytes accessed | tf_op | source)
XLA Modules:
  0.0 132.9 jit_solution(6748553456306091714)
XLA Ops:
  1.6 1.2 shard_map.121
  2.8 5.6 %all-to-all-start = ((bf16[16,32,1408]{2,1,0:T(8,128)(2,1)}), bf16[16,32,1408]{2,1,0:T(8,128)(2,1)S(1)}, u32[]{:S(2)}, u32[]{:S(2)}) async-start(bf16[16,32,1408]{2,1,0:T(8,128)(2,1)} %shard_map.121), calls=%async_computation | async-start | bytes 2883584 | tf_op jit(solution)/shard_map/all_to_all | solution.py:451
  8.4 2.3 %collective-permute-start = (bf16[264,1408]{1,0:T(8,128)(2,1)}, bf16[264,1408]{1,0:T(8,128)(2,1)}, u32[]{:S(2)}, u32[]{:S(2)}) collective-permute-start(bf16[264,1408]{1,0:T(8,128)(2,1)} %bitcast.11), channel_id=1, source_target_pairs={{0,32},{32,0},{64,96},{96,64},{128,160},{160,128},{192,224},{224,1... | collective-permute-start | bytes 2230280 | tf_op jit(solution)/shard_map/ppermute | solution.py:454
  10.7 2.0 %collective-permute-start.3 = (bf16[264,1408]{1,0:T(8,128)(2,1)}, bf16[264,1408]{1,0:T(8,128)(2,1)}, u32[]{:S(2)}, u32[]{:S(2)}) collective-permute-start(bf16[264,1408]{1,0:T(8,128)(2,1)} %bitcast.13), channel_id=1, source_target_pairs={{0,32},{32,0},{64,96},{96,64},{128,160},{160,128},{192,224},{224,1... | collective-permute-start | bytes 2230280 | tf_op jit(solution)/shard_map/ppermute | solution.py:455
  12.7 2.3 %collective-permute-start.1 = (bf16[88,1408]{1,0:T(8,128)(2,1)S(1)}, bf16[88,1408]{1,0:T(8,128)(2,1)S(1)}, u32[]{:S(2)}, u32[]{:S(2)}) collective-permute-start(bf16[88,1408]{1,0:T(8,128)(2,1)S(1)} %copy-done.9), channel_id=1, source_target_pairs={{0,32},{32,0},{64,96},{96,64},{128,160},{160,128},{192,224},{224,1... | collective-permute-start | bytes 743432 | tf_op jit(solution)/shard_map/ppermute | solution.py:456
  15.1 2.0 %collective-permute-start.2 = (bf16[88,1408]{1,0:T(8,128)(2,1)S(1)}, bf16[88,1408]{1,0:T(8,128)(2,1)S(1)}, u32[]{:S(2)}, u32[]{:S(2)}) collective-permute-start(bf16[88,1408]{1,0:T(8,128)(2,1)S(1)} %copy-done.1), channel_id=1, source_target_pairs={{0,32},{32,0},{64,96},{96,64},{128,160},{160,128},{192,224},{224,1... | collective-permute-start | bytes 743432 | tf_op jit(solution)/shard_map/ppermute | solution.py:457
  20.6 1.9 %shard_map.122 = (f32[2,88,256]{2,1,0:T(8,128)S(1)}, f32[2,88,256]{2,1,0:T(8,128)S(1)}, f32[1,256]{1,0:T(1,128)S(1)}, f32[4,256]{1,0:T(4,128)S(1)}, f32[4,1408]{...) custom-call(s32[4,8]{1,0:T(4,128)S(1)} %bitcast.10, s32[1]{0:T(128)} %bitcast.frame, ...), custom_call_target="tpu_custom_call" | custom-call | tf_op jit(solution)/shard_map/pallas_call | solution.py:52
  23.9 5.3 %all-to-all-done.x = bf16[16,32,1408]{2,1,0:T(8,128)(2,1)S(1)} async-done(((bf16[16,32,1408]{2,1,0:T(8,128)(2,1)}), bf16[16,32,1408]{2,1,0:T(8,128)(2,1)S(1)}, u32[]{:S(2)}, u32[]{:S(2)}) %all-to-all-start) | async-done | bytes 1441824 | tf_op jit(solution)/shard_map/all_to_all | solution.py:451
  29.2 5.7 %shard_map.123 = (bf16[4,128,1408]{2,1,0:T(8,128)(2,1)S(1)}, f32[4,1,256]{2,1,0:T(1,128)}) custom-call(bf16[16,32,1408]{2,1,0:T(8,128)(2,1)S(1)} %all-to-all-done.x, bf16[264,1408]{1,0:T(8,128)(2,1)} %bitcast.12, bf16[264,1408]{1,0:T(8,128)(2,1)} %collective-permute-done.w_oth_far, f32[2,88,256]{2,1,0:T(8,128)} %copy-done.12, f32[1,256]{1,0:T(1,128)S(1)} %get-tuple-element.30.otz), custom_call_target="tpu_custom_call" | custom-call | tf_op jit(solution)/shard_map/pallas_call | solution.py:52
  34.9 6.5 %all-to-all-start.1 = ((f32[4,1,256]{2,1,0:T(1,128)}), f32[4,1,256]{2,1,0:T(1,128)S(1)}, u32[]{:S(2)}, u32[]{:S(2)}) async-start(f32[4,1,256]{2,1,0:T(1,128)} %get-tuple-element.38), calls=%async_computation.1 | async-start | bytes 8192 | tf_op jit(solution)/shard_map/all_to_all | solution.py:480
  41.5 6.5 %shard_map.124 = (bf16[3,4,128,88]{3,2,1,0:T(8,128)(2,1)}, bf16[3,4,128,88]{3,2,1,0:T(8,128)(2,1)}, f32[4,4,136,128]{3,2,1,0:T(8,128)}, f32[4,4,136,128]{3,2,1,0...) custom-call(bf16[4,128,1408]{2,1,0:T(8,128)(2,1)S(1)} %get-tuple-element.51.normed, ...), custom_call_target="tpu_custom_call" | custom-call | tf_op jit(solution)/shard_map/pallas_call | solution.py:52
  48.1 1.6 %shard_map.127.flip_own_far = bf16[1408,512]{1,0:T(8,128)(2,1)} custom-call(bf16[4,128,1408]{2,1,0:T(8,128)(2,1)S(1)} %get-tuple-element.51.normed), custom_call_target="tpu_custom_call" | custom-call | tf_op jit(solution)/shard_map/pallas_call | solution.py:52
  49.7 2.1 %collective-permute-start.6 = (bf16[1408,512]{1,0:T(8,128)(2,1)}, bf16[1408,512]{1,0:T(8,128)(2,1)}, u32[]{:S(2)}, u32[]{:S(2)}) collective-permute-start(bf16[1408,512]{1,0:T(8,128)(2,1)} %shard_map.127.flip_own_far), channel_id=1, source_target_pairs={{0,32},{32,0},{64,96},{96,64},{128,160},{160,128},{192,224},{224,1... | collective-permute-start | bytes 4325384 | tf_op jit(solution)/shard_map/ppermute | solution.py:515
  51.7 2.4 %collective-permute-start.5 = (f32[4,4,136,128]{3,2,1,0:T(8,128)}, f32[4,4,136,128]{3,2,1,0:T(8,128)S(1)}, u32[]{:S(2)}, u32[]{:S(2)}) collective-permute-start(f32[4,4,136,128]{3,2,1,0:T(8,128)} %get-tuple-element.50), channel_id=1, source_target_pairs={{0,32},{32,0},{64,96},{96,64},{128,160},{160,128},{192,224},{224,1... | collective-permute-start | bytes 3342344 | tf_op jit(solution)/shard_map/ppermute | solution.py:516
  54.2 9.9 %all_to_all.25.got = f32[16,24,128]{2,1,0:T(8,128)S(1)} all-to-all(f32[16,24,128]{2,1,0:T(8,128)S(1)} %shard_map.125), channel_id=1, replica_groups=mesh['frame'=16,'crop'=4,'dp'=8] {'frame'}, dimensions={0} | all-to-all | bytes 393216 | tf_op jit(solution)/shard_map/all_to_all | solution.py:507
  64.1 2.2 %shard_map.126 = (f32[16,24,128]{2,1,0:T(8,128)}, f32[4,256]{1,0:T(4,128)S(1)}, f32[4,88]{1,0:T(4,128)S(1)}) custom-call(f32[16,24,128]{2,1,0:T(8,128)S(1)} %all_to_all.25.got, bf16[256,2048]{1,0:T(8,128)(2,1)S(1)} %copy-done, f32[1,2048]{1,0:T(1,128)S(1)} %bitcast.9), custom_call_target="tpu_custom_call" | custom-call | tf_op jit(solution)/shard_map/pallas_call | solution.py:52
  66.3 3.5 %all-to-all-start.3 = ((f32[16,24,128]{2,1,0:T(8,128)}), f32[16,24,128]{2,1,0:T(8,128)S(1)}, u32[]{:S(2)}, u32[]{:S(2)}) async-start(f32[16,24,128]{2,1,0:T(8,128)} %get-tuple-element.44), calls=%async_computation.3 | async-start | bytes 393216 | tf_op jit(solution)/shard_map/all_to_all | solution.py:523
  69.9 2.4 %collective-permute-start.4 = (bf16[3,4,128,88]{3,2,1,0:T(8,128)(2,1)S(1)}, bf16[3,4,128,88]{3,2,1,0:T(8,128)(2,1)S(1)}, u32[]{:S(2)}, u32[]{:S(2)}) collective-permute-start(bf16[3,4,128,88]{3,2,1,0:T(8,128)(2,1)S(1)} %copy-done.15), channel_id=1, source_target_pairs={{0,32},{32,0},{64,96},{96,64},{128,160},{160,128},{192,224},{224,1... | collective-permute-start | bytes 811016 | tf_op jit(solution)/shard_map/ppermute | solution.py:517
  72.2 1.2 collective-permute-done.4.oth_far
  73.5 3.7 %all-to-all-done.3.got = f32[16,24,128]{2,1,0:T(8,128)S(1)} async-done(((f32[16,24,128]{2,1,0:T(8,128)}), f32[16,24,128]{2,1,0:T(8,128)S(1)}, u32[]{:S(2)}, u32[]{:S(2)}) %all-to-all-start.3) | async-done | bytes 196640 | tf_op jit(solution)/shard_map/all_to_all | solution.py:523
  77.1 11.8 %shard_map.128 = s16[32,56,256]{2,1,0:T(8,128)(2,1)} custom-call(f32[16,24,128]{2,1,0:T(8,128)S(1)} %all-to-all-done.3.got, f32[4,256]{1,0:T(4,128)S(1)} %get-tuple-element.45.zs, f32[4,88]{1,0:T(4,128)S(1)} %get-tuple-element.46.heads, f32[2,88,256]{2,1,0:T(8,128)S(1)} %copy-done.8, bf16[3,4,128,88]{3,2,1,0:T(8,128)(2,1)} %get-tuple-element.47.own_far, ...), custom_call_target="tpu_custom_call" | custom-call | tf_op jit(solution)/shard_map/pallas_call | solution.py:52
  88.9 15.0 %all-to-all-start.4 = ((s16[32,56,256]{2,1,0:T(8,128)(2,1)}), s16[32,56,256]{2,1,0:T(8,128)(2,1)S(1)}, u32[]{:S(2)}, u32[]{:S(2)}) async-start(s16[32,56,256]{2,1,0:T(8,128)(2,1)} %shard_map.128), calls=%async_computation.4 | async-start | bytes 1835008 | tf_op jit(solution)/shard_map/all_to_all | solution.py:541
  104.7 26.8 %all-to-all-done.4.got = s16[32,56,256]{2,1,0:T(8,128)(2,1)S(1)} async-done(((s16[32,56,256]{2,1,0:T(8,128)(2,1)}), s16[32,56,256]{2,1,0:T(8,128)(2,1)S(1)}, u32[]{:S(2)}, u32[]{:S(2)}) %all-to-all-start.4) | async-done | bytes 917536 | tf_op jit(solution)/shard_map/all_to_all | solution.py:541
  131.4 1.5 %shard_map.129 = (f32[44,264]{1,0:T(8,128)}, f32[44,88]{1,0:T(8,128)}, f32[44,256]{1,0:T(8,128)}) custom-call(s16[32,56,256]{2,1,0:T(8,128)(2,1)S(1)} %all-to-all-done.4.got, bf16[44,256]{1,0:T(8,128)(2,1)S(1)} %constant_dynamic-slice_fusion.bottle), custom_call_target="tpu_custom_call" | custom-call | tf_op jit(solution)/shard_map/pallas_call | solution.py:52
  (41 shorter events, 6.7 us)
Async XLA Ops:
  0.6 0.9 copy-start.4
  2.8 9.9 %copy-start.9 = (bf16[88,1408]{1,0:T(8,128)(2,1)S(1)}, bf16[88,1408]{1,0:T(8,128)(2,1)}, u32[]{:S(2)}) copy-start(bf16[88,1408]{1,0:T(8,128)(2,1)} %t_out.1) | copy-start | bytes 743428
  2.8 12.3 %copy-start.1 = (bf16[88,1408]{1,0:T(8,128)(2,1)S(1)}, bf16[88,1408]{1,0:T(8,128)(2,1)}, u32[]{:S(2)}) copy-start(bf16[88,1408]{1,0:T(8,128)(2,1)} %s_out_far.1) | copy-start | bytes 743428
  2.8 15.7 %copy-start.3 = (bf16[1408,256]{1,0:T(8,128)(2,1)S(1)}, bf16[1408,256]{1,0:T(8,128)(2,1)}, u32[]{:S(2)}) copy-start(bf16[1408,256]{1,0:T(8,128)(2,1)} %s_bot.1) | copy-start | bytes 2162692
  2.8 15.7 %copy-start.5 = (bf16[1,1,64,1408]{3,2,1,0:T(8,128)(2,1)S(1)}, bf16[1,1,64,1408]{3,2,1,0:T(8,128)(2,1)}, u32[]{:S(2)}) copy-start(bf16[1,1,64,1408]{3,2,1,0:T(8,128)(2,1)} %param.10) | copy-start | bytes 540676
  2.8 15.7 %copy-start.14 = (s32[1,4,8]{2,1,0:T(4,128)S(1)}, s32[1,4,8]{2,1,0:T(4,128)}, u32[]{:S(2)}) copy-start(s32[1,4,8]{2,1,0:T(4,128)} %param.11) | copy-start | bytes 388
  2.8 26.4 %all-to-all-start = ((bf16[16,32,1408]{2,1,0:T(8,128)(2,1)}), bf16[16,32,1408]{2,1,0:T(8,128)(2,1)S(1)}, u32[]{:S(2)}, u32[]{:S(2)}) async-start(bf16[16,32,1408]{2,1,0:T(8,128)(2,1)} %shard_map.121), calls=%async_computation | async-start | bytes 2883584 | tf_op jit(solution)/shard_map/all_to_all | solution.py:451
  8.4 15.5 %collective-permute-start = (bf16[264,1408]{1,0:T(8,128)(2,1)}, bf16[264,1408]{1,0:T(8,128)(2,1)}, u32[]{:S(2)}, u32[]{:S(2)}) collective-permute-start(bf16[264,1408]{1,0:T(8,128)(2,1)} %bitcast.11), channel_id=1, source_target_pairs={{0,32},{32,0},{64,96},{96,64},{128,160},{160,128},{192,224},{224,1... | collective-permute-start | bytes 2230280 | tf_op jit(solution)/shard_map/ppermute | solution.py:454
  10.7 30.8 %collective-permute-start.3 = (bf16[264,1408]{1,0:T(8,128)(2,1)}, bf16[264,1408]{1,0:T(8,128)(2,1)}, u32[]{:S(2)}, u32[]{:S(2)}) collective-permute-start(bf16[264,1408]{1,0:T(8,128)(2,1)} %bitcast.13), channel_id=1, source_target_pairs={{0,32},{32,0},{64,96},{96,64},{128,160},{160,128},{192,224},{224,1... | collective-permute-start | bytes 2230280 | tf_op jit(solution)/shard_map/ppermute | solution.py:455
  12.7 4.4 %collective-permute-start.1 = (bf16[88,1408]{1,0:T(8,128)(2,1)S(1)}, bf16[88,1408]{1,0:T(8,128)(2,1)S(1)}, u32[]{:S(2)}, u32[]{:S(2)}) collective-permute-start(bf16[88,1408]{1,0:T(8,128)(2,1)S(1)} %copy-done.9), channel_id=1, source_target_pairs={{0,32},{32,0},{64,96},{96,64},{128,160},{160,128},{192,224},{224,1... | collective-permute-start | bytes 743432 | tf_op jit(solution)/shard_map/ppermute | solution.py:456
  15.1 3.4 %collective-permute-start.2 = (bf16[88,1408]{1,0:T(8,128)(2,1)S(1)}, bf16[88,1408]{1,0:T(8,128)(2,1)S(1)}, u32[]{:S(2)}, u32[]{:S(2)}) collective-permute-start(bf16[88,1408]{1,0:T(8,128)(2,1)S(1)} %copy-done.1), channel_id=1, source_target_pairs={{0,32},{32,0},{64,96},{96,64},{128,160},{160,128},{192,224},{224,1... | collective-permute-start | bytes 743432 | tf_op jit(solution)/shard_map/ppermute | solution.py:457
  18.5 10.7 %copy-start.2 = (bf16[88,1408]{1,0:T(8,128)(2,1)}, bf16[88,1408]{1,0:T(8,128)(2,1)S(1)}, u32[]{:S(2)}) copy-start(bf16[88,1408]{1,0:T(8,128)(2,1)S(1)} %collective-permute-done.2.s_oth.s_oth_far) | copy-start | bytes 743428
  18.5 1.2 copy-start.6
  19.7 0.9 copy-start.11
  34.9 13.0 %all-to-all-start.1 = ((f32[4,1,256]{2,1,0:T(1,128)}), f32[4,1,256]{2,1,0:T(1,128)S(1)}, u32[]{:S(2)}, u32[]{:S(2)}) async-start(f32[4,1,256]{2,1,0:T(1,128)} %get-tuple-element.38), calls=%async_computation.1 | async-start | bytes 8192 | tf_op jit(solution)/shard_map/all_to_all | solution.py:480
  48.1 16.0 %copy-start = (bf16[256,2048]{1,0:T(8,128)(2,1)S(1)}, bf16[256,2048]{1,0:T(8,128)(2,1)}, u32[]{:S(2)}) copy-start(bf16[256,2048]{1,0:T(8,128)(2,1)} %protos.1) | copy-start | bytes 3145732
  48.1 16.0 %copy-start.13 = (f32[2048]{0:T(1024)S(1)}, f32[2048]{0:T(1024)}, u32[]{:S(2)}) copy-start(f32[2048]{0:T(1024)} %param.19) | copy-start | bytes 24580
  49.7 20.2 %copy-start.15 = (bf16[3,4,128,88]{3,2,1,0:T(8,128)(2,1)S(1)}, bf16[3,4,128,88]{3,2,1,0:T(8,128)(2,1)}, u32[]{:S(2)}) copy-start(bf16[3,4,128,88]{3,2,1,0:T(8,128)(2,1)} %get-tuple-element.48) | copy-start | bytes 811012
  49.7 27.5 %copy-start.8 = (f32[2,88,256]{2,1,0:T(8,128)S(1)}, f32[2,88,256]{2,1,0:T(8,128)}, u32[]{:S(2)}) copy-start(f32[2,88,256]{2,1,0:T(8,128)} %copy-done.7) | copy-start | bytes 540676
  49.7 27.5 %collective-permute-start.6 = (bf16[1408,512]{1,0:T(8,128)(2,1)}, bf16[1408,512]{1,0:T(8,128)(2,1)}, u32[]{:S(2)}, u32[]{:S(2)}) collective-permute-start(bf16[1408,512]{1,0:T(8,128)(2,1)} %shard_map.127.flip_own_far), channel_id=1, source_target_pairs={{0,32},{32,0},{64,96},{96,64},{128,160},{160,128},{192,224},{224,1... | collective-permute-start | bytes 4325384 | tf_op jit(solution)/shard_map/ppermute | solution.py:515
  51.7 25.4 %collective-permute-start.5 = (f32[4,4,136,128]{3,2,1,0:T(8,128)}, f32[4,4,136,128]{3,2,1,0:T(8,128)S(1)}, u32[]{:S(2)}, u32[]{:S(2)}) collective-permute-start(f32[4,4,136,128]{3,2,1,0:T(8,128)} %get-tuple-element.50), channel_id=1, source_target_pairs={{0,32},{32,0},{64,96},{96,64},{128,160},{160,128},{192,224},{224,1... | collective-permute-start | bytes 3342344 | tf_op jit(solution)/shard_map/ppermute | solution.py:516
  66.3 10.8 %all-to-all-start.3 = ((f32[16,24,128]{2,1,0:T(8,128)}), f32[16,24,128]{2,1,0:T(8,128)S(1)}, u32[]{:S(2)}, u32[]{:S(2)}) async-start(f32[16,24,128]{2,1,0:T(8,128)} %get-tuple-element.44), calls=%async_computation.3 | async-start | bytes 393216 | tf_op jit(solution)/shard_map/all_to_all | solution.py:523
  69.9 3.6 %collective-permute-start.4 = (bf16[3,4,128,88]{3,2,1,0:T(8,128)(2,1)S(1)}, bf16[3,4,128,88]{3,2,1,0:T(8,128)(2,1)S(1)}, u32[]{:S(2)}, u32[]{:S(2)}) collective-permute-start(bf16[3,4,128,88]{3,2,1,0:T(8,128)(2,1)S(1)} %copy-done.15), channel_id=1, source_target_pairs={{0,32},{32,0},{64,96},{96,64},{128,160},{160,128},{192,224},{224,1... | collective-permute-start | bytes 811016 | tf_op jit(solution)/shard_map/ppermute | solution.py:517
  88.9 42.5 %all-to-all-start.4 = ((s16[32,56,256]{2,1,0:T(8,128)(2,1)}), s16[32,56,256]{2,1,0:T(8,128)(2,1)S(1)}, u32[]{:S(2)}, u32[]{:S(2)}) async-start(s16[32,56,256]{2,1,0:T(8,128)(2,1)} %shard_map.128), calls=%async_computation.4 | async-start | bytes 1835008 | tf_op jit(solution)/shard_map/all_to_all | solution.py:541
  (3 other events, 2.0 us)

commit v3 on v2

--- a/solution.py
+++ b/solution.py
@@ -111,10 +111,17 @@
     return [rows[:, head * PITCH + part * HS : head * PITCH + (part + 1) * HS].astype(BF16) for part in range(3)]
 
 
-def spread_kernel(tok, out):
-    half = out.shape[1]
-    for peer in range(FRAMES):
-        out[peer] = tok[(peer % 2) * half : (peer % 2 + 1) * half, :]
+def spread_kernel(tok_far, out_far, tok, sems, out_sems):
+    (copy,) = begin((tok_far,), (tok,), sems)
+    copy.wait()
+    half = out_far.shape[1]
+    leaving = begin(
+        [tok.at[pl.ds((peer % 2) * half, half)] for peer in range(FRAMES)],
+        [out_far.at[peer] for peer in range(FRAMES)],
+        out_sems,
+    )
+    for copy in leaving:
+        copy.wait()
 
 
 def prep_kernel(
@@ -447,6 +454,7 @@
         spread_kernel,
         [((FRAMES, tokens.shape[0] // 2, D), BF16)],
         tokens,
+        hbm_in=(0,), hbm_out=(0,), scratch=room(tokens) + [pltpu.SemaphoreType.DMA((FRAMES,))],
     )
     mixed = lax.all_to_all(spread, "frame", 0, 0, tiled=True)
     t_own = teacher_qkv.T

time: 134 us -> 134 us (level)
  the two profiles are of different devices: /device:TPU:80 before, /device:TPU:16 now
where the time goes in v3:
time: 134 us; the launch traced here: 133 us
  starting transfers between devices  47 us (35%)
  waiting for transfers between devices  36.7 us (27%)
  Pallas kernels  33.6 us (25%)
  blocking collectives  9.92 us (7%)
  local copies, waits for them, and re-layouts  4.97 us (4%)
    pallas_call x9, Pallas kernels, call(): pl.pallas_call(kernel, out_shape=tuple((pltpu.HBM(shape, dtype) if index...  33.6 us
    all_to_all x1, waiting for transfers between devices, local(): got = lax.all_to_all(sent, ('crop', 'dp'), 0, 0, tiled=True)  25.9 us
    all_to_all x1, starting transfers between devices, local(): got = lax.all_to_all(sent, ('crop', 'dp'), 0, 0, tiled=True)  15.2 us
    all_to_all x1, blocking collectives, local(): got = lax.all_to_all(sent, 'frame', 0, 0, tiled=True)  9.92 us
    all_to_all x1, starting transfers between devices, local(): ztc = lax.all_to_all(zt, 'crop', 0, 0, tiled=True)  7.17 us
    all_to_all x1, starting transfers between devices, local(): mixed = lax.all_to_all(spread, 'frame', 0, 0, tiled=True)  5.56 us
    all_to_all x1, waiting for transfers between devices, local(): mixed = lax.all_to_all(spread, 'frame', 0, 0, tiled=True)  5.24 us
    unnamed x30, local copies, waits for them, and re-layouts  4.2 us
  transfers between devices with their start and end apart: 11, of which 5 were waited for; matrix products, arithmetic and copies ran while one was open for 1% of the time, Pallas kernels for 12%

profile of v3, /device:TPU:16, one launch (start us, length us, event | category | flops | bytes accessed | tf_op | source)
XLA Modules:
  0.0 133.1 jit_solution(17028244046867572824)
XLA Ops:
  0.6 2.2 %shard_map.121 = bf16[16,32,1408]{2,1,0:T(8,128)(2,1)} custom-call(bf16[64,1408]{1,0:T(8,128)(2,1)} %bitcast.7), custom_call_target="tpu_custom_call" | custom-call | tf_op jit(solution)/shard_map/pallas_call | solution.py:52
  2.9 5.6 %all-to-all-start = ((bf16[16,32,1408]{2,1,0:T(8,128)(2,1)}), bf16[16,32,1408]{2,1,0:T(8,128)(2,1)S(1)}, u32[]{:S(2)}, u32[]{:S(2)}) async-start(bf16[16,32,1408]{2,1,0:T(8,128)(2,1)} %shard_map.121), calls=%async_computation | async-start | bytes 2883584 | tf_op jit(solution)/shard_map/all_to_all | solution.py:459
  8.5 2.3 %collective-permute-start = (bf16[264,1408]{1,0:T(8,128)(2,1)}, bf16[264,1408]{1,0:T(8,128)(2,1)}, u32[]{:S(2)}, u32[]{:S(2)}) collective-permute-start(bf16[264,1408]{1,0:T(8,128)(2,1)} %bitcast.11), channel_id=1, source_target_pairs={{0,32},{32,0},{64,96},{96,64},{128,160},{160,128},{192,224},{224,1... | collective-permute-start | bytes 2230280 | tf_op jit(solution)/shard_map/ppermute | solution.py:462
  10.8 2.0 %collective-permute-start.3 = (bf16[264,1408]{1,0:T(8,128)(2,1)}, bf16[264,1408]{1,0:T(8,128)(2,1)}, u32[]{:S(2)}, u32[]{:S(2)}) collective-permute-start(bf16[264,1408]{1,0:T(8,128)(2,1)} %bitcast.13), channel_id=1, source_target_pairs={{0,32},{32,0},{64,96},{96,64},{128,160},{160,128},{192,224},{224,1... | collective-permute-start | bytes 2230280 | tf_op jit(solution)/shard_map/ppermute | solution.py:463
  12.8 2.3 %collective-permute-start.1 = (bf16[88,1408]{1,0:T(8,128)(2,1)S(1)}, bf16[88,1408]{1,0:T(8,128)(2,1)S(1)}, u32[]{:S(2)}, u32[]{:S(2)}) collective-permute-start(bf16[88,1408]{1,0:T(8,128)(2,1)S(1)} %copy-done.8), channel_id=1, source_target_pairs={{0,32},{32,0},{64,96},{96,64},{128,160},{160,128},{192,224},{224,1... | collective-permute-start | bytes 743432 | tf_op jit(solution)/shard_map/ppermute | solution.py:464
  15.2 2.0 %collective-permute-start.2 = (bf16[88,1408]{1,0:T(8,128)(2,1)S(1)}, bf16[88,1408]{1,0:T(8,128)(2,1)S(1)}, u32[]{:S(2)}, u32[]{:S(2)}) collective-permute-start(bf16[88,1408]{1,0:T(8,128)(2,1)S(1)} %copy-done.1), channel_id=1, source_target_pairs={{0,32},{32,0},{64,96},{96,64},{128,160},{160,128},{192,224},{224,1... | collective-permute-start | bytes 743432 | tf_op jit(solution)/shard_map/ppermute | solution.py:465
  20.7 1.9 %shard_map.122 = (f32[2,88,256]{2,1,0:T(8,128)S(1)}, f32[2,88,256]{2,1,0:T(8,128)S(1)}, f32[1,256]{1,0:T(1,128)S(1)}, f32[4,256]{1,0:T(4,128)S(1)}, f32[4,1408]{...) custom-call(s32[4,8]{1,0:T(4,128)S(1)} %bitcast.10, s32[1]{0:T(128)} %bitcast.frame, ...), custom_call_target="tpu_custom_call" | custom-call | tf_op jit(solution)/shard_map/pallas_call | solution.py:52
  24.0 5.2 %all-to-all-done.x = bf16[16,32,1408]{2,1,0:T(8,128)(2,1)S(1)} async-done(((bf16[16,32,1408]{2,1,0:T(8,128)(2,1)}), bf16[16,32,1408]{2,1,0:T(8,128)(2,1)S(1)}, u32[]{:S(2)}, u32[]{:S(2)}) %all-to-all-start) | async-done | bytes 1441824 | tf_op jit(solution)/shard_map/all_to_all | solution.py:459
  29.3 5.7 %shard_map.123 = (bf16[4,128,1408]{2,1,0:T(8,128)(2,1)S(1)}, f32[4,1,256]{2,1,0:T(1,128)}) custom-call(bf16[16,32,1408]{2,1,0:T(8,128)(2,1)S(1)} %all-to-all-done.x, bf16[264,1408]{1,0:T(8,128)(2,1)} %bitcast.12, bf16[264,1408]{1,0:T(8,128)(2,1)} %collective-permute-done.w_oth_far, f32[2,88,256]{2,1,0:T(8,128)} %copy-done.11, f32[1,256]{1,0:T(1,128)S(1)} %get-tuple-element.30.otz), custom_call_target="tpu_custom_call" | custom-call | tf_op jit(solution)/shard_map/pallas_call | solution.py:52
  35.0 7.2 %all-to-all-start.1 = ((f32[4,1,256]{2,1,0:T(1,128)}), f32[4,1,256]{2,1,0:T(1,128)S(1)}, u32[]{:S(2)}, u32[]{:S(2)}) async-start(f32[4,1,256]{2,1,0:T(1,128)} %get-tuple-element.38), calls=%async_computation.1 | async-start | bytes 8192 | tf_op jit(solution)/shard_map/all_to_all | solution.py:488
  42.2 6.5 %shard_map.124 = (bf16[3,4,128,88]{3,2,1,0:T(8,128)(2,1)}, bf16[3,4,128,88]{3,2,1,0:T(8,128)(2,1)}, f32[4,4,136,128]{3,2,1,0:T(8,128)}, f32[4,4,136,128]{3,2,1,0...) custom-call(bf16[4,128,1408]{2,1,0:T(8,128)(2,1)S(1)} %get-tuple-element.51.normed, ...), custom_call_target="tpu_custom_call" | custom-call | tf_op jit(solution)/shard_map/pallas_call | solution.py:52
  48.8 1.6 %shard_map.127.flip_own_far = bf16[1408,512]{1,0:T(8,128)(2,1)} custom-call(bf16[4,128,1408]{2,1,0:T(8,128)(2,1)S(1)} %get-tuple-element.51.normed), custom_call_target="tpu_custom_call" | custom-call | tf_op jit(solution)/shard_map/pallas_call | solution.py:52
  50.4 2.1 %collective-permute-start.6 = (bf16[1408,512]{1,0:T(8,128)(2,1)}, bf16[1408,512]{1,0:T(8,128)(2,1)}, u32[]{:S(2)}, u32[]{:S(2)}) collective-permute-start(bf16[1408,512]{1,0:T(8,128)(2,1)} %shard_map.127.flip_own_far), channel_id=1, source_target_pairs={{0,32},{32,0},{64,96},{96,64},{128,160},{160,128},{192,224},{224,1... | collective-permute-start | bytes 4325384 | tf_op jit(solution)/shard_map/ppermute | solution.py:523
  52.5 2.4 %collective-permute-start.5 = (f32[4,4,136,128]{3,2,1,0:T(8,128)}, f32[4,4,136,128]{3,2,1,0:T(8,128)S(1)}, u32[]{:S(2)}, u32[]{:S(2)}) collective-permute-start(f32[4,4,136,128]{3,2,1,0:T(8,128)} %get-tuple-element.50), channel_id=1, source_target_pairs={{0,32},{32,0},{64,96},{96,64},{128,160},{160,128},{192,224},{224,1... | collective-permute-start | bytes 3342344 | tf_op jit(solution)/shard_map/ppermute | solution.py:524
  54.9 9.9 %all_to_all.25.got = f32[16,24,128]{2,1,0:T(8,128)S(1)} all-to-all(f32[16,24,128]{2,1,0:T(8,128)S(1)} %shard_map.125), channel_id=1, replica_groups=mesh['frame'=16,'crop'=4,'dp'=8] {'frame'}, dimensions={0} | all-to-all | bytes 393216 | tf_op jit(solution)/shard_map/all_to_all | solution.py:515
  64.8 2.2 %shard_map.126 = (f32[16,24,128]{2,1,0:T(8,128)}, f32[4,256]{1,0:T(4,128)S(1)}, f32[4,88]{1,0:T(4,128)S(1)}) custom-call(f32[16,24,128]{2,1,0:T(8,128)S(1)} %all_to_all.25.got, bf16[256,2048]{1,0:T(8,128)(2,1)S(1)} %copy-done, f32[1,2048]{1,0:T(1,128)S(1)} %bitcast.9), custom_call_target="tpu_custom_call" | custom-call | tf_op jit(solution)/shard_map/pallas_call | solution.py:52
  67.1 3.5 %all-to-all-start.3 = ((f32[16,24,128]{2,1,0:T(8,128)}), f32[16,24,128]{2,1,0:T(8,128)S(1)}, u32[]{:S(2)}, u32[]{:S(2)}) async-start(f32[16,24,128]{2,1,0:T(8,128)} %get-tuple-element.44), calls=%async_computation.3 | async-start | bytes 393216 | tf_op jit(solution)/shard_map/all_to_all | solution.py:531
  70.6 2.4 %collective-permute-start.4 = (bf16[3,4,128,88]{3,2,1,0:T(8,128)(2,1)S(1)}, bf16[3,4,128,88]{3,2,1,0:T(8,128)(2,1)S(1)}, u32[]{:S(2)}, u32[]{:S(2)}) collective-permute-start(bf16[3,4,128,88]{3,2,1,0:T(8,128)(2,1)S(1)} %copy-done.14), channel_id=1, source_target_pairs={{0,32},{32,0},{64,96},{96,64},{128,160},{160,128},{192,224},{224,1... | collective-permute-start | bytes 811016 | tf_op jit(solution)/shard_map/ppermute | solution.py:525
  73.0 1.2 collective-permute-done.4.oth_far
  74.2 3.7 %all-to-all-done.3.got = f32[16,24,128]{2,1,0:T(8,128)S(1)} async-done(((f32[16,24,128]{2,1,0:T(8,128)}), f32[16,24,128]{2,1,0:T(8,128)S(1)}, u32[]{:S(2)}, u32[]{:S(2)}) %all-to-all-start.3) | async-done | bytes 196640 | tf_op jit(solution)/shard_map/all_to_all | solution.py:531
  77.9 11.8 %shard_map.128 = s16[32,56,256]{2,1,0:T(8,128)(2,1)} custom-call(f32[16,24,128]{2,1,0:T(8,128)S(1)} %all-to-all-done.3.got, f32[4,256]{1,0:T(4,128)S(1)} %get-tuple-element.45.zs, f32[4,88]{1,0:T(4,128)S(1)} %get-tuple-element.46.heads, f32[2,88,256]{2,1,0:T(8,128)S(1)} %copy-done.7, bf16[3,4,128,88]{3,2,1,0:T(8,128)(2,1)} %get-tuple-element.47.own_far, ...), custom_call_target="tpu_custom_call" | custom-call | tf_op jit(solution)/shard_map/pallas_call | solution.py:52
  89.7 15.2 %all-to-all-start.4 = ((s16[32,56,256]{2,1,0:T(8,128)(2,1)}), s16[32,56,256]{2,1,0:T(8,128)(2,1)S(1)}, u32[]{:S(2)}, u32[]{:S(2)}) async-start(s16[32,56,256]{2,1,0:T(8,128)(2,1)} %shard_map.128), calls=%async_computation.4 | async-start | bytes 1835008 | tf_op jit(solution)/shard_map/all_to_all | solution.py:549
  105.7 25.9 %all-to-all-done.4.got = s16[32,56,256]{2,1,0:T(8,128)(2,1)S(1)} async-done(((s16[32,56,256]{2,1,0:T(8,128)(2,1)}), s16[32,56,256]{2,1,0:T(8,128)(2,1)S(1)}, u32[]{:S(2)}, u32[]{:S(2)}) %all-to-all-start.4) | async-done | bytes 917536 | tf_op jit(solution)/shard_map/all_to_all | solution.py:549
  131.6 1.5 %shard_map.129 = (f32[44,264]{1,0:T(8,128)}, f32[44,88]{1,0:T(8,128)}, f32[44,256]{1,0:T(8,128)}) custom-call(s16[32,56,256]{2,1,0:T(8,128)(2,1)S(1)} %all-to-all-done.4.got, bf16[44,256]{1,0:T(8,128)(2,1)S(1)} %constant_dynamic-slice_fusion.bottle), custom_call_target="tpu_custom_call" | custom-call | tf_op jit(solution)/shard_map/pallas_call | solution.py:52
  (39 shorter events, 5.8 us)
Async XLA Ops:
  2.9 10.0 %copy-start.8 = (bf16[88,1408]{1,0:T(8,128)(2,1)S(1)}, bf16[88,1408]{1,0:T(8,128)(2,1)}, u32[]{:S(2)}) copy-start(bf16[88,1408]{1,0:T(8,128)(2,1)} %t_out.1) | copy-start | bytes 743428
  2.9 12.3 %copy-start.1 = (bf16[88,1408]{1,0:T(8,128)(2,1)S(1)}, bf16[88,1408]{1,0:T(8,128)(2,1)}, u32[]{:S(2)}) copy-start(bf16[88,1408]{1,0:T(8,128)(2,1)} %s_out_far.1) | copy-start | bytes 743428
  2.9 15.7 %copy-start.3 = (bf16[1408,256]{1,0:T(8,128)(2,1)S(1)}, bf16[1408,256]{1,0:T(8,128)(2,1)}, u32[]{:S(2)}) copy-start(bf16[1408,256]{1,0:T(8,128)(2,1)} %s_bot.1) | copy-start | bytes 2162692
  2.9 15.7 %copy-start.4 = (bf16[1,1,64,1408]{3,2,1,0:T(8,128)(2,1)S(1)}, bf16[1,1,64,1408]{3,2,1,0:T(8,128)(2,1)}, u32[]{:S(2)}) copy-start(bf16[1,1,64,1408]{3,2,1,0:T(8,128)(2,1)} %param.10) | copy-start | bytes 540676
  2.9 15.7 %copy-start.13 = (s32[1,4,8]{2,1,0:T(4,128)S(1)}, s32[1,4,8]{2,1,0:T(4,128)}, u32[]{:S(2)}) copy-start(s32[1,4,8]{2,1,0:T(4,128)} %param.11) | copy-start | bytes 388
  2.9 26.4 %all-to-all-start = ((bf16[16,32,1408]{2,1,0:T(8,128)(2,1)}), bf16[16,32,1408]{2,1,0:T(8,128)(2,1)S(1)}, u32[]{:S(2)}, u32[]{:S(2)}) async-start(bf16[16,32,1408]{2,1,0:T(8,128)(2,1)} %shard_map.121), calls=%async_computation | async-start | bytes 2883584 | tf_op jit(solution)/shard_map/all_to_all | solution.py:459
  8.5 15.5 %collective-permute-start = (bf16[264,1408]{1,0:T(8,128)(2,1)}, bf16[264,1408]{1,0:T(8,128)(2,1)}, u32[]{:S(2)}, u32[]{:S(2)}) collective-permute-start(bf16[264,1408]{1,0:T(8,128)(2,1)} %bitcast.11), channel_id=1, source_target_pairs={{0,32},{32,0},{64,96},{96,64},{128,160},{160,128},{192,224},{224,1... | collective-permute-start | bytes 2230280 | tf_op jit(solution)/shard_map/ppermute | solution.py:462
  10.8 31.4 %collective-permute-start.3 = (bf16[264,1408]{1,0:T(8,128)(2,1)}, bf16[264,1408]{1,0:T(8,128)(2,1)}, u32[]{:S(2)}, u32[]{:S(2)}) collective-permute-start(bf16[264,1408]{1,0:T(8,128)(2,1)} %bitcast.13), channel_id=1, source_target_pairs={{0,32},{32,0},{64,96},{96,64},{128,160},{160,128},{192,224},{224,1... | collective-permute-start | bytes 2230280 | tf_op jit(solution)/shard_map/ppermute | solution.py:463
  12.8 4.4 %collective-permute-start.1 = (bf16[88,1408]{1,0:T(8,128)(2,1)S(1)}, bf16[88,1408]{1,0:T(8,128)(2,1)S(1)}, u32[]{:S(2)}, u32[]{:S(2)}) collective-permute-start(bf16[88,1408]{1,0:T(8,128)(2,1)S(1)} %copy-done.8), channel_id=1, source_target_pairs={{0,32},{32,0},{64,96},{96,64},{128,160},{160,128},{192,224},{224,1... | collective-permute-start | bytes 743432 | tf_op jit(solution)/shard_map/ppermute | solution.py:464
  15.2 3.4 %collective-permute-start.2 = (bf16[88,1408]{1,0:T(8,128)(2,1)S(1)}, bf16[88,1408]{1,0:T(8,128)(2,1)S(1)}, u32[]{:S(2)}, u32[]{:S(2)}) collective-permute-start(bf16[88,1408]{1,0:T(8,128)(2,1)S(1)} %copy-done.1), channel_id=1, source_target_pairs={{0,32},{32,0},{64,96},{96,64},{128,160},{160,128},{192,224},{224,1... | collective-permute-start | bytes 743432 | tf_op jit(solution)/shard_map/ppermute | solution.py:465
  17.2 0.7 copy-start.9
  18.6 10.7 %copy-start.2 = (bf16[88,1408]{1,0:T(8,128)(2,1)}, bf16[88,1408]{1,0:T(8,128)(2,1)S(1)}, u32[]{:S(2)}) copy-start(bf16[88,1408]{1,0:T(8,128)(2,1)S(1)} %collective-permute-done.2.s_oth.s_oth_far) | copy-start | bytes 743428
  18.6 1.2 copy-start.5
  19.8 0.9 copy-start.10
  35.0 13.7 %all-to-all-start.1 = ((f32[4,1,256]{2,1,0:T(1,128)}), f32[4,1,256]{2,1,0:T(1,128)S(1)}, u32[]{:S(2)}, u32[]{:S(2)}) async-start(f32[4,1,256]{2,1,0:T(1,128)} %get-tuple-element.38), calls=%async_computation.1 | async-start | bytes 8192 | tf_op jit(solution)/shard_map/all_to_all | solution.py:488
  48.8 16.0 %copy-start = (bf16[256,2048]{1,0:T(8,128)(2,1)S(1)}, bf16[256,2048]{1,0:T(8,128)(2,1)}, u32[]{:S(2)}) copy-start(bf16[256,2048]{1,0:T(8,128)(2,1)} %protos.1) | copy-start | bytes 3145732
  48.8 16.0 %copy-start.12 = (f32[2048]{0:T(1024)S(1)}, f32[2048]{0:T(1024)}, u32[]{:S(2)}) copy-start(f32[2048]{0:T(1024)} %param.19) | copy-start | bytes 24580
  50.4 20.2 %copy-start.14 = (bf16[3,4,128,88]{3,2,1,0:T(8,128)(2,1)S(1)}, bf16[3,4,128,88]{3,2,1,0:T(8,128)(2,1)}, u32[]{:S(2)}) copy-start(bf16[3,4,128,88]{3,2,1,0:T(8,128)(2,1)} %get-tuple-element.48) | copy-start | bytes 811012
  50.4 27.5 %copy-start.7 = (f32[2,88,256]{2,1,0:T(8,128)S(1)}, f32[2,88,256]{2,1,0:T(8,128)}, u32[]{:S(2)}) copy-start(f32[2,88,256]{2,1,0:T(8,128)} %copy-done.6) | copy-start | bytes 540676
  50.4 27.5 %collective-permute-start.6 = (bf16[1408,512]{1,0:T(8,128)(2,1)}, bf16[1408,512]{1,0:T(8,128)(2,1)}, u32[]{:S(2)}, u32[]{:S(2)}) collective-permute-start(bf16[1408,512]{1,0:T(8,128)(2,1)} %shard_map.127.flip_own_far), channel_id=1, source_target_pairs={{0,32},{32,0},{64,96},{96,64},{128,160},{160,128},{192,224},{224,1... | collective-permute-start | bytes 4325384 | tf_op jit(solution)/shard_map/ppermute | solution.py:523
  52.5 25.4 %collective-permute-start.5 = (f32[4,4,136,128]{3,2,1,0:T(8,128)}, f32[4,4,136,128]{3,2,1,0:T(8,128)S(1)}, u32[]{:S(2)}, u32[]{:S(2)}) collective-permute-start(f32[4,4,136,128]{3,2,1,0:T(8,128)} %get-tuple-element.50), channel_id=1, source_target_pairs={{0,32},{32,0},{64,96},{96,64},{128,160},{160,128},{192,224},{224,1... | collective-permute-start | bytes 3342344 | tf_op jit(solution)/shard_map/ppermute | solution.py:524
  67.1 10.8 %all-to-all-start.3 = ((f32[16,24,128]{2,1,0:T(8,128)}), f32[16,24,128]{2,1,0:T(8,128)S(1)}, u32[]{:S(2)}, u32[]{:S(2)}) async-start(f32[16,24,128]{2,1,0:T(8,128)} %get-tuple-element.44), calls=%async_computation.3 | async-start | bytes 393216 | tf_op jit(solution)/shard_map/all_to_all | solution.py:531
  70.6 3.6 %collective-permute-start.4 = (bf16[3,4,128,88]{3,2,1,0:T(8,128)(2,1)S(1)}, bf16[3,4,128,88]{3,2,1,0:T(8,128)(2,1)S(1)}, u32[]{:S(2)}, u32[]{:S(2)}) collective-permute-start(bf16[3,4,128,88]{3,2,1,0:T(8,128)(2,1)S(1)} %copy-done.14), channel_id=1, source_target_pairs={{0,32},{32,0},{64,96},{96,64},{128,160},{160,128},{192,224},{224,1... | collective-permute-start | bytes 811016 | tf_op jit(solution)/shard_map/ppermute | solution.py:525
  89.7 41.9 %all-to-all-start.4 = ((s16[32,56,256]{2,1,0:T(8,128)(2,1)}), s16[32,56,256]{2,1,0:T(8,128)(2,1)S(1)}, u32[]{:S(2)}, u32[]{:S(2)}) async-start(s16[32,56,256]{2,1,0:T(8,128)(2,1)} %shard_map.128), calls=%async_computation.4 | async-start | bytes 1835008 | tf_op jit(solution)/shard_map/all_to_all | solution.py:549
  (2 other events, 1.3 us)
